TPU v7x, 256 devices: a whole 4x4x8 slice. The times are simulated.
256 devices in a mesh: sens: 8 (over x_lo, y), pts: 32 (over z, x_hi, core).
Axes of the slice: x: 4 (x_hi: 2, x_lo: 2; x = x_hi * 2 + x_lo), y: 4, z: 8, core: 2. Of those that a mesh axis runs over, the one named last changes fastest.
Arguments:
- vectors: float32 [4, 1024, 420], P(None, 'pts'), may hold values from -6 to 6
- kernel_hat: float32 [2, 448, 512, 1024], P(None, 'pts', 'sens'), may hold values from -0.1875 to 0.1875
- noise_prec: float32 [512], P(('sens', 'pts')), may hold values from 0.3 to 3
- stencil_coefficients_raw: float32 [1024, 6], P('pts'), may hold values from 0.1 to 2
- offsets: int32 [1024, 6], P('pts'), may hold values from -32 to 32
- amplitude: float32 [1024], P('pts'), may hold values from 0.5 to 2
- cheb_coef: float32 [5], replicated, may hold values from 0.2 to 1
Outputs:
- hess_vec: float32 [4, 1024, 420], P(None, 'pts')
Inputs may be any that keep to these rules, and one draw needn't show every extreme that they name: `offsets`: each point's stencil neighbours lie at most 32 points away in the point order.
All inputs are finite; a program needn't handle non-finite values.
Results may differ from a plain program's by a relative error of at most 0.00016.
Values sent between devices are 32-bit elements; how exact they have to be, the bound alone decides.
No kernel may reach another device: no remote copies, remote signals or barrier semaphores. Data moves between devices by JAX's collectives and lax.ppermute only.
A program may use at most 64 MiB of HBM per device.

v0:
```python
import numpy as np
import jax
import jax.numpy as jnp
from jax import lax
from jax.experimental import pallas as pl
from jax.experimental.pallas import tpu as pltpu
from jax.sharding import PartitionSpec as P

LANES = 128
SPAN = 256
REACH = 64
SLOTS = 16


def spare_lane(item):
    return 32 * (item // 4) + 28 + item % 4


def halves(values):
    high = values.astype(jnp.bfloat16)
    low = (values - high.astype(jnp.float32)).astype(jnp.bfloat16)
    return high, low


def host_halves(values):
    values = values.astype(np.float32)
    high = values.astype(jnp.bfloat16)
    low = (values - high.astype(np.float32)).astype(jnp.bfloat16)
    return high, low


def tables(length, block, blocks, padded_time):
    time = np.arange(length)

    def angle(frequency):
        return np.pi / length * ((frequency[:, None] * time[None, :]) % (2 * length))

    base = angle(np.arange(blocks) * block)
    coarse = np.zeros((blocks, 2, padded_time))
    coarse[:, 0, :length] = np.cos(base)
    coarse[:, 1, :length] = np.sin(base)
    coarse = coarse.reshape(blocks, 2 * padded_time)
    fine_angle = angle(np.arange(block))
    fine = np.zeros((2, SLOTS, 2, padded_time))
    fine[0, :block, 0, :length] = np.cos(fine_angle)
    fine[0, :block, 1, :length] = -np.sin(fine_angle)
    fine[1, :block, 0, :length] = -np.sin(fine_angle)
    fine[1, :block, 1, :length] = -np.cos(fine_angle)
    fine = fine.reshape(2, 2 * SLOTS, padded_time)
    full_angle = angle(np.arange(blocks * block)).reshape(blocks, block, length)
    full = np.zeros((padded_time, blocks, SLOTS, 2))
    full[:length, :, :block, 0] = np.cos(full_angle).transpose(2, 0, 1)
    full[:length, :, :block, 1] = -np.sin(full_angle).transpose(2, 0, 1)
    full = full.reshape(padded_time, blocks * 2 * SLOTS)
    coarse_high, coarse_low = host_halves(coarse)
    to_time = np.concatenate([coarse_high, coarse_high, coarse_low, coarse_low], axis=0)
    to_frequency = np.concatenate([coarse_high, coarse_low], axis=0).T.copy()
    full_high, full_low = host_halves(full)
    return full_high, full_low, to_time, to_frequency, fine.astype(np.float32)


def dot(a, b):
    return jnp.dot(a, b, preferred_element_type=jnp.float32)


def iota(shape, axis):
    return lax.broadcasted_iota(jnp.int32, shape, axis)


def source_kernel(vectors, raw, offsets, amplitude, full_high, full_low, out, padded, items):
    count, points, length = vectors.shape
    padded[...] = jnp.zeros_like(padded)
    for v in range(count):
        padded[v * points : (v + 1) * points, :length] = vectors[v]
    items[...] = jnp.zeros_like(items)
    near = raw.shape[0]
    weights = raw[...] / jnp.sum(raw[...], axis=0, keepdims=True)
    shifts = offsets[...].astype(jnp.float32)
    for k in range(near):
        lane = spare_lane(k)
        items[lane : lane + 1, :points] = weights[k : k + 1]
        lane = spare_lane(near + k)
        items[lane : lane + 1, :points] = shifts[k : k + 1]
    lane = spare_lane(2 * near)
    items[lane : lane + 1, :points] = amplitude[...]
    extra = items[...].T[:points]
    rows = count * points
    high, low = halves(padded[...])
    both = jnp.concatenate([high, low], axis=0)
    group_of_lane = iota((points, LANES), 1) // 32
    width = SPAN
    for start in range(0, full_high.shape[1], width):
        first = dot(both, full_high[:, start : start + width])
        second = dot(high, full_low[:, start : start + width])
        spectrum = first[:rows] + first[rows:] + second
        for tile in range(width // LANES):
            part = spectrum[:, tile * LANES : (tile + 1) * LANES]
            for e in range(4):
                block = extra
                for v in range(count):
                    piece = part[v * points : (v + 1) * points]
                    shift = (32 * (v - e)) % LANES
                    if shift:
                        piece = pltpu.roll(piece, shift, 1)
                    block = block + jnp.where(group_of_lane == v, piece, 0.0)
                out[start // 32 + tile * 4 + e] = block


def chebyshev(load, store, band, coef, previous, current, total, state):
    points = total.shape[0]
    rows = LANES
    blocks = points // rows
    edge = jnp.zeros((REACH, SPAN), jnp.bfloat16)
    for parity in range(2):
        state[parity, :REACH] = edge
        state[parity, REACH + points :] = edge

    def put(parity, b, values):
        high, low = halves(values)
        state[parity, REACH + b * rows : REACH + (b + 1) * rows, :LANES] = high
        state[parity, REACH + b * rows : REACH + (b + 1) * rows, LANES:] = low

    for b in range(blocks):
        at = slice(b * rows, (b + 1) * rows)
        values = load(b)
        previous[at] = values
        total[at] = coef[0] * values
        put(0, b, values)
    degree = coef.shape[0] - 1
    for j in range(1, degree + 1):
        for b in range(blocks):
            at = slice(b * rows, (b + 1) * rows)
            product = dot(band[b], state[(j - 1) % 2, b * rows : b * rows + SPAN])
            moved = product[:rows, :LANES] + product[:rows, LANES:] + product[rows:, :LANES]
            if j == 1:
                values = moved
            else:
                values = 2.0 * moved - previous[at]
                if j < degree:
                    previous[at] = current[at]
            if j < degree:
                current[at] = values
                total[at] = total[at] + coef[j] * values
                put(j % 2, b, values)
            else:
                store(b, total[at] + coef[j] * values)


def put_band(band, b, matrix):
    high, low = halves(matrix)
    band[b, :LANES] = high
    band[b, LANES:] = low


def item(table, index):
    lane = spare_lane(index)
    return table[:, lane : lane + 1]


def lane_frequency(shape):
    return (iota(shape, 1) % 32) // 2


def swapped(values):
    real = iota(values.shape, 1) % 2 == 0
    following = pltpu.roll(values, LANES - 1, 1)
    leading = pltpu.roll(values, 1, 1)
    return real, following, leading


def forward_kernel(near, received, coef, kernel, out, band, previous, current, total, state, ready, held, sems):
    pairs = sems.shape[0]
    copies = []
    for g in range(pairs):
        copy = pltpu.make_async_copy(kernel.at[:, pl.ds(2 * g, 2)], held.at[:, pl.ds(2 * g, 2)], sems.at[g])
        copy.start()
        copies.append(copy)
    points = total.shape[0]
    column = iota((LANES, SPAN), 1).astype(jnp.float32)
    row = iota((LANES, 1), 0).astype(jnp.float32)
    for b in range(points // LANES):
        table = received[b * LANES : (b + 1) * LANES]
        matrix = jnp.zeros((LANES, SPAN), jnp.float32)
        for k in range(near):
            target = item(table, near + k) + (row + float(REACH))
            matrix = matrix + jnp.where(column == target, item(table, k), 0.0)
        put_band(band, b, matrix)

    def load(b):
        return received[b * LANES : (b + 1) * LANES]

    def store(b, values):
        at = slice(b * LANES, (b + 1) * LANES)
        high, low = halves(item(received[at], 2 * near) * values)
        ready[at, :LANES] = high
        ready[at, LANES:] = low

    chebyshev(load, store, band, coef, previous, current, total, state)
    sensors = out.shape[0]
    of_lane = lane_frequency((sensors, LANES))
    direct = jnp.zeros((sensors, LANES), jnp.float32)
    crossed = jnp.zeros((sensors, LANES), jnp.float32)
    for g in range(pairs):
        copies[g].wait()
        parts = []
        for f in (2 * g, 2 * g + 1):
            for c in range(2):
                parts.extend(halves(held[c, f]))
        product = dot(jnp.concatenate(parts, axis=0), ready[...])
        for n, f in enumerate((2 * g, 2 * g + 1)):
            sums = []
            for c in range(2):
                at = (2 * n + c) * 2 * sensors
                top = product[at : at + sensors]
                bottom = product[at + sensors : at + 2 * sensors]
                sums.append(top[:, :LANES] + top[:, LANES:] + bottom[:, :LANES])
            direct = jnp.where(of_lane == f, sums[0], direct)
            crossed = jnp.where(of_lane == f, sums[1], crossed)
    real, following, leading = swapped(crossed)
    out[...] = direct + jnp.where(real, -following, leading)


def frequency_weight(block, blocks, length):
    shape = (blocks, LANES)
    slot = lane_frequency(shape)
    frequency = iota(shape, 0) * block + slot
    edge = (frequency == 0) | (frequency == length)
    weight = jnp.where(edge, 0.5 / length, 1.0 / length).astype(jnp.float32)
    return jnp.where((slot < block) & (frequency <= length), weight, 0.0)


def series(received, sets, blocks, weight, to_time, fine, each):
    padded_time = fine.shape[2]
    stacked = []
    for n in range(sets):
        values = received[pl.ds(n, blocks, stride=sets), :] * weight
        high = values.astype(jnp.bfloat16).astype(jnp.float32)
        low = values - high
        stacked.append(jnp.concatenate([high, low, high, low], axis=0).T.astype(jnp.bfloat16))
    product = dot(jnp.concatenate(stacked, axis=0), to_time[...])
    for n in range(sets):
        for v in range(4):
            at = n * LANES + v * 32
            rows = product[at : at + 32]
            terms = rows[:, :padded_time] * fine[0] + rows[:, padded_time:] * fine[1]
            each(n, v, jnp.sum(terms, axis=0, keepdims=True))


def sensor_kernel(block, length, received, noise, to_time, to_frequency, fine, out, moved):
    blocks = out.shape[0] // 2
    padded_time = fine.shape[2]
    weight = frequency_weight(block, blocks, length)

    def each(n, v, values):
        weighted = values * noise[n]
        for half in range(2):
            high, low = halves(weighted * fine[half])
            at = slice(half * padded_time, (half + 1) * padded_time)
            moved[n * SPAN + v * 32 : n * SPAN + v * 32 + 32, at] = high
            moved[n * SPAN + LANES + v * 32 : n * SPAN + LANES + v * 32 + 32, at] = low

    series(received, 2, blocks, weight, to_time, fine, each)
    product = dot(moved[...], to_frequency[...])
    for n in range(2):
        high = product[n * SPAN : n * SPAN + LANES]
        low = product[n * SPAN + LANES : (n + 1) * SPAN]
        result = high[:, :blocks] + high[:, blocks:] + low[:, :blocks]
        out[pl.ds(n, blocks, stride=2), :] = result.T


def adjoint_kernel(near, received, table, coef, kernel, out, band, previous, current, total, state, flat, held, stencil, sems):
    chunks = sems.shape[0]
    copies = []
    for n in range(chunks):
        at = pl.ds(n * SPAN, SPAN)
        copy = pltpu.make_async_copy(kernel.at[:, :, :, at], held.at[:, :, :, at], sems.at[n])
        copy.start()
        copies.append(copy)
    points = total.shape[0]
    blocks = points // LANES
    stencil[...] = jnp.zeros_like(stencil)
    for b in range(blocks):
        turned = table[b * LANES : (b + 1) * LANES].T
        for m in range(2 * near):
            lane = spare_lane(m)
            stencil[m : m + 1, (b + 1) * LANES : (b + 2) * LANES] = turned[lane : lane + 1]
    row = iota((LANES, SPAN), 0).astype(jnp.float32)
    column = iota((1, SPAN), 1).astype(jnp.float32) - float(REACH)
    for b in range(blocks):
        window = pltpu.roll(stencil[:, b * LANES : (b + 3) * LANES], 3 * LANES - REACH, 1)[:, :SPAN]
        matrix = jnp.zeros((LANES, SPAN), jnp.float32)
        for k in range(near):
            target = window[near + k : near + k + 1] + column
            matrix = matrix + jnp.where(row == target, window[k : k + 1], 0.0)
        put_band(band, b, matrix)
    sensors = received.shape[0]
    values = received[...]
    real, following, leading = swapped(values)
    turned = jnp.concatenate([values, jnp.where(real, following, -leading)], axis=0).T
    high, low = halves(turned)
    both = jnp.concatenate([high, low], axis=0)
    of_row = ((iota((2 * LANES, LANES), 0) % 32) // 2)
    frequencies = kernel.shape[1]
    spread = jnp.concatenate(
        [jnp.where(of_row == f, both, jnp.zeros_like(both)) for f in range(frequencies)], axis=1
    )
    for n in range(chunks):
        copies[n].wait()
        highs, lows = [], []
        for f in range(frequencies):
            for c in range(2):
                a, b = halves(held[c, f, :, n * SPAN : (n + 1) * SPAN])
                highs.append(a)
                lows.append(b)
        first = dot(spread, jnp.concatenate(highs, axis=0))
        second = dot(spread[:LANES], jnp.concatenate(lows, axis=0))
        flat[n * SPAN : (n + 1) * SPAN] = (first[:LANES] + first[LANES:] + second).T

    def load(b):
        at = slice(b * LANES, (b + 1) * LANES)
        return item(table[at], 2 * near) * flat[at]

    def store(b, values):
        for i in range(4):
            for j in range(8):
                at = 16 * b + 4 * i
                out[j, at : at + 4] = values[32 * i + 4 * j : 32 * i + 4 * j + 4]

    chebyshev(load, store, band, coef, previous, current, total, state)


def gradient_kernel(block, length, received, to_time, fine, out, once):
    blocks = received.shape[0] // 4
    weight = frequency_weight(block, blocks, length)

    def each(n, v, values):
        for tile in range(values.shape[1] // LANES):
            at = 16 * tile + 4 * v + n
            once[at : at + 1] = values[:, tile * LANES : (tile + 1) * LANES]

    series(received, 4, blocks, weight, to_time, fine, each)
    for copy in range(out.shape[0]):
        out[copy] = once[...]


def final_kernel(received, vectors, out):
    count, _, length = out.shape
    groups = received.shape[0]
    for tile in range(received.shape[1] // 16):
        lanes = min(LANES, length - tile * LANES)
        at = slice(tile * LANES, tile * LANES + lanes)
        for v in range(count):
            rows = [received[j, 16 * tile + 4 * v : 16 * tile + 4 * v + 4] for j in range(groups)]
            out[v, :, at] = vectors[v, :, at] + jnp.concatenate(rows, axis=0)[:, :lanes]


VMEM = pl.BlockSpec(memory_space=pltpu.VMEM)
SMEM = pl.BlockSpec(memory_space=pltpu.SMEM)
ANY = pl.BlockSpec(memory_space=pl.ANY)


def call(kernel, name, shape, specs, scratch=()):
    return pl.pallas_call(
        kernel,
        name=name,
        out_shape=jax.ShapeDtypeStruct(shape, jnp.float32),
        in_specs=specs,
        out_specs=VMEM,
        scratch_shapes=list(scratch),
    )


def exchange(values, axis):
    return lax.all_to_all(values, axis, 0, 0, tiled=True)


def body(vectors, kernel_hat, noise_prec, stencil_coefficients_raw, offsets, amplitude, cheb_coef):
    from functools import partial

    count, points, length = vectors.shape
    _, block, sensors, all_points = kernel_hat.shape
    near = offsets.shape[1]
    blocks = lax.axis_size("pts")
    groups = lax.axis_size("sens")
    padded_time = 512
    full_high, full_low, to_time, to_frequency, fine = tables(length, block, blocks, padded_time)
    f32, bf16 = jnp.float32, jnp.bfloat16
    grid_scratch = [
        pltpu.VMEM((all_points // LANES, SPAN, SPAN), bf16),
        pltpu.VMEM((all_points, LANES), f32),
        pltpu.VMEM((all_points, LANES), f32),
        pltpu.VMEM((all_points, LANES), f32),
        pltpu.VMEM((2, all_points + 2 * REACH, SPAN), bf16),
    ]
    source = call(
        source_kernel,
        "source",
        (blocks, points, LANES),
        [VMEM] * 6,
        [pltpu.VMEM((count * points, padded_time), f32), pltpu.VMEM((LANES, LANES), f32)],
    )(vectors, stencil_coefficients_raw.T, offsets.T, amplitude.reshape(1, points), full_high, full_low)
    spectrum = exchange(source, "pts").reshape(all_points, LANES)
    data = call(
        partial(forward_kernel, near),
        "forward",
        (sensors, LANES),
        [VMEM, SMEM, ANY],
        grid_scratch
        + [
            pltpu.VMEM((all_points, SPAN), bf16),
            pltpu.VMEM(kernel_hat.shape, f32),
            pltpu.SemaphoreType.DMA((block // 2,)),
        ],
    )(spectrum, cheb_coef, kernel_hat)
    data = exchange(data.reshape(blocks, sensors // blocks, LANES), "pts").reshape(sensors, LANES)
    back = call(
        partial(sensor_kernel, block, length),
        "sensor",
        (sensors, LANES),
        [VMEM, SMEM, VMEM, VMEM, VMEM],
        [pltpu.VMEM((2 * SPAN, 2 * padded_time), bf16)],
    )(data, noise_prec, to_time, to_frequency, fine)
    back = exchange(back.reshape(blocks, sensors // blocks, LANES), "pts").reshape(sensors, LANES)
    partial_sums = call(
        partial(adjoint_kernel, near),
        "adjoint",
        (groups, all_points // groups, LANES),
        [VMEM, VMEM, SMEM, ANY],
        grid_scratch
        + [
            pltpu.VMEM((all_points, LANES), f32),
            pltpu.VMEM(kernel_hat.shape, f32),
            pltpu.VMEM((SLOTS, all_points + 2 * LANES), f32),
            pltpu.SemaphoreType.DMA((all_points // SPAN,)),
        ],
    )(back, spectrum, cheb_coef, kernel_hat)
    summed = jnp.sum(exchange(partial_sums, "sens"), axis=0)
    share = points // groups
    moved = exchange(summed.reshape(blocks, share, LANES), "pts").reshape(blocks * share, LANES)
    gradient = call(
        partial(gradient_kernel, block, length),
        "gradient",
        (groups, share * count * padded_time // LANES, LANES),
        [VMEM, VMEM, VMEM],
        [pltpu.VMEM((share * count * padded_time // LANES, LANES), f32)],
    )(moved, to_time, fine)
    gathered = exchange(gradient, "sens")
    return call(final_kernel, "final", (count, points, length), [VMEM, VMEM])(gathered, vectors)


def solution(mesh):
    placed = (
        P(None, "pts", None),
        P(None, "pts", "sens", None),
        P(("sens", "pts")),
        P("pts", None),
        P("pts", None),
        P("pts"),
        P(),
    )
    return jax.shard_map(
        body, mesh=mesh, in_specs=placed, out_specs=P(None, "pts", None), check_vma=False
    )
```

profile of v0, /device:TPU:1, one launch (start us, length us, event | category | flops | bytes accessed | tf_op | source)
XLA Modules:
  0.0 126.5 jit_solution(12543468028399538654)
XLA Ops:
  0.0 3.3 %source.1 = f32[32,32,128]{2,1,0:T(8,128)} custom-call(f32[4,32,420]{2,1,0:T(8,128)} %vectors.3, f32[6,32]{1,0:T(8,128)} %bitcast.18, s32[6,32]{1,0:T(8,128)} %bitcast.19, f32[1,32]{1,0:T(1,128)} %bitcast.20, bf16[512,1024]{1,0:T(8,128)(2,1)} %constant.12.clone.full_high, bf16[512,1024]{1,0:T(8,128)(2,1)} %constant.13.clone.full_low), custom_call_target="tpu_custom_call" | custom-call | tf_op jit(solution)/shard_map/source/pallas_call | solution.py:395
  3.3 29.5 %all_to_all.30 = f32[32,32,128]{2,1,0:T(8,128)} all-to-all(f32[32,32,128]{2,1,0:T(8,128)} %source.1), channel_id=1, replica_groups=mesh['sens'=8,'pts'=32] {'pts'}, dimensions={0} | all-to-all | bytes 1048576 | tf_op jit(solution)/shard_map/all_to_all | solution.py:374
  32.9 10.2 %forward.1 = f32[64,128]{1,0:T(8,128)} custom-call(f32[1024,128]{1,0:T(8,128)} %bitcast.10, f32[5]{0:T(128)} %coef.3, f32[2,14,64,1024]{3,2,1,0:T(8,128)} %kernel.3), custom_call_target="tpu_custom_call" | custom-call | tf_op jit(solution)/shard_map/forward/pallas_call | solution.py:403
  43.1 15.6 %all_to_all.31 = f32[32,2,128]{2,1,0:T(2,128)} all-to-all(f32[32,2,128]{2,1,0:T(2,128)} %bitcast.15), channel_id=1, replica_groups=mesh['sens'=8,'pts'=32] {'pts'}, dimensions={0} | all-to-all | bytes 65536 | tf_op jit(solution)/shard_map/all_to_all | solution.py:374
  58.6 2.5 %sensor.1 = f32[64,128]{1,0:T(8,128)} custom-call(f32[64,128]{1,0:T(8,128)} %bitcast.16, f32[2]{0:T(128)} %noise.1, bf16[128,1024]{1,0:T(8,128)(2,1)} %constant.14.clone.to_time, bf16[1024,64]{1,0:T(8,128)(2,1)} %constant.15.clone.to_frequency, f32[2,32,512]{2,1,0:T(8,128)} %constant.16.clone.fine), custom_call_target="tpu_custom_call" | custom-call | tf_op jit(solution)/shard_map/sensor/pallas_call | solution.py:416
  61.1 14.3 %all_to_all.32 = f32[32,2,128]{2,1,0:T(2,128)} all-to-all(f32[32,2,128]{2,1,0:T(2,128)} %bitcast.17), channel_id=1, replica_groups=mesh['sens'=8,'pts'=32] {'pts'}, dimensions={0} | all-to-all | bytes 65536 | tf_op jit(solution)/shard_map/all_to_all | solution.py:374
  75.5 8.3 %adjoint.1 = f32[8,128,128]{2,1,0:T(8,128)} custom-call(f32[64,128]{1,0:T(8,128)} %bitcast.14, f32[1024,128]{1,0:T(8,128)} %bitcast.11, f32[5]{0:T(128)} %coef.3, f32[2,14,64,1024]{3,2,1,0:T(8,128)} %kernel.3), custom_call_target="tpu_custom_call" | custom-call | tf_op jit(solution)/shard_map/adjoint/pallas_call | solution.py:424
  83.8 13.0 %all_to_all.33 = f32[8,128,128]{2,1,0:T(8,128)S(1)} all-to-all(f32[8,128,128]{2,1,0:T(8,128)} %adjoint.1), channel_id=1, replica_groups=mesh['sens'=8,'pts'=32] {'sens'}, dimensions={0} | all-to-all | bytes 1048576 | tf_op jit(solution)/shard_map/all_to_all | solution.py:374
  96.8 15.4 %all_to_all.34 = f32[32,4,128]{2,1,0:T(4,128)} all-to-all(f32[32,4,128]{2,1,0:T(4,128)S(1)} %bitcast.13), channel_id=1, replica_groups=mesh['sens'=8,'pts'=32] {'pts'}, dimensions={0} | all-to-all | bytes 131072 | tf_op jit(solution)/shard_map/all_to_all | solution.py:374
  112.2 2.3 %gradient.1 = f32[8,64,128]{2,1,0:T(8,128)} custom-call(f32[128,128]{1,0:T(8,128)} %bitcast.12, bf16[128,1024]{1,0:T(8,128)(2,1)} %constant.14.clone.to_time, f32[2,32,512]{2,1,0:T(8,128)} %constant.16.clone.fine), custom_call_target="tpu_custom_call" | custom-call | tf_op jit(solution)/shard_map/gradient/pallas_call | solution.py:440
  114.5 10.1 %all_to_all.35.received = f32[8,64,128]{2,1,0:T(8,128)} all-to-all(f32[8,64,128]{2,1,0:T(8,128)} %gradient.1), channel_id=1, replica_groups=mesh['sens'=8,'pts'=32] {'sens'}, dimensions={0} | all-to-all | bytes 524288 | tf_op jit(solution)/shard_map/all_to_all | solution.py:374
  124.7 1.8 %final.1 = f32[4,32,420]{2,1,0:T(8,128)} custom-call(f32[8,64,128]{2,1,0:T(8,128)} %all_to_all.35.received, f32[4,32,420]{2,1,0:T(8,128)} %vectors.3), custom_call_target="tpu_custom_call" | custom-call | tf_op jit(solution)/shard_map/final/pallas_call | solution.py:448
  (1 shorter events, 0.0 us)
where the time goes:
time: 127 us; the launch traced here: 126 us
  blocking collectives  98 us (77%)
  Pallas kernels  28.4 us (22%)
    all_to_all x6, blocking collectives, exchange(): return lax.all_to_all(values, axis, 0, 0, tiled=True)  98 us
    pallas_call x1, Pallas kernels, body(): call(partial(forward_kernel, near), 'forward', (sensors, LANES), [VMEM, S...  10.2 us
    pallas_call x1, Pallas kernels, body(): call(partial(adjoint_kernel, near), 'adjoint', (groups, all_points // gro...  8.28 us
    pallas_call x1, Pallas kernels, body(): call(source_kernel, 'source', (blocks, points, LANES), [VMEM] * 6, [pltpu...  3.33 us

commit v1 on v0

--- a/solution.py
+++ b/solution.py
@@ -168,7 +168,9 @@
     return real, following, leading
 
 
-def forward_kernel(near, received, coef, kernel, out, band, previous, current, total, state, ready, held, sems):
+def forward_kernel(
+    near, received, coef, kernel, out, highs, lows, band, previous, current, total, state, ready, held, sems
+):
     pairs = sems.shape[0]
     copies = []
     for g in range(pairs):
@@ -205,7 +207,10 @@
         parts = []
         for f in (2 * g, 2 * g + 1):
             for c in range(2):
-                parts.extend(halves(held[c, f]))
+                high, low = halves(held[c, f])
+                highs[c, f] = high
+                lows[c, f] = low
+                parts.extend((high, low))
         product = dot(jnp.concatenate(parts, axis=0), ready[...])
         for n, f in enumerate((2 * g, 2 * g + 1)):
             sums = []
@@ -268,14 +273,9 @@
         out[pl.ds(n, blocks, stride=2), :] = result.T
 
 
-def adjoint_kernel(near, received, table, coef, kernel, out, band, previous, current, total, state, flat, held, stencil, sems):
-    chunks = sems.shape[0]
-    copies = []
-    for n in range(chunks):
-        at = pl.ds(n * SPAN, SPAN)
-        copy = pltpu.make_async_copy(kernel.at[:, :, :, at], held.at[:, :, :, at], sems.at[n])
-        copy.start()
-        copies.append(copy)
+def adjoint_kernel(near, received, table, coef, highs, lows, out, band, previous, current, total, state, flat, stencil):
+    chunks = highs.shape[3] // SPAN
+    frequencies = highs.shape[1]
     points = total.shape[0]
     blocks = points // LANES
     stencil[...] = jnp.zeros_like(stencil)
@@ -300,20 +300,14 @@
     high, low = halves(turned)
     both = jnp.concatenate([high, low], axis=0)
     of_row = ((iota((2 * LANES, LANES), 0) % 32) // 2)
-    frequencies = kernel.shape[1]
     spread = jnp.concatenate(
         [jnp.where(of_row == f, both, jnp.zeros_like(both)) for f in range(frequencies)], axis=1
     )
     for n in range(chunks):
-        copies[n].wait()
-        highs, lows = [], []
-        for f in range(frequencies):
-            for c in range(2):
-                a, b = halves(held[c, f, :, n * SPAN : (n + 1) * SPAN])
-                highs.append(a)
-                lows.append(b)
-        first = dot(spread, jnp.concatenate(highs, axis=0))
-        second = dot(spread[:LANES], jnp.concatenate(lows, axis=0))
+        at = slice(n * SPAN, (n + 1) * SPAN)
+        order = [(c, f) for f in range(frequencies) for c in range(2)]
+        first = dot(spread, jnp.concatenate([highs[c, f, :, at] for c, f in order], axis=0))
+        second = dot(spread[:LANES], jnp.concatenate([lows[c, f, :, at] for c, f in order], axis=0))
         flat[n * SPAN : (n + 1) * SPAN] = (first[:LANES] + first[LANES:] + second).T
 
     def load(b):
@@ -356,22 +350,35 @@
 
 VMEM = pl.BlockSpec(memory_space=pltpu.VMEM)
 SMEM = pl.BlockSpec(memory_space=pltpu.SMEM)
-ANY = pl.BlockSpec(memory_space=pl.ANY)
-
-
-def call(kernel, name, shape, specs, scratch=()):
+HBM = pl.BlockSpec(memory_space=pltpu.HBM)
+
+
+def call(kernel, name, shapes, specs, scratch=(), fast=True):
+    def result(shape, kind):
+        return pltpu.VMEM(shape, kind) if fast else jax.ShapeDtypeStruct(shape, kind)
+
+    outs = [result(shape, kind) for shape, kind in shapes]
     return pl.pallas_call(
         kernel,
         name=name,
-        out_shape=jax.ShapeDtypeStruct(shape, jnp.float32),
+        out_shape=outs if len(outs) > 1 else outs[0],
         in_specs=specs,
-        out_specs=VMEM,
+        out_specs=[VMEM] * len(outs) if len(outs) > 1 else VMEM,
         scratch_shapes=list(scratch),
+        compiler_params=pltpu.CompilerParams(vmem_limit_bytes=28 * 1024 * 1024),
     )
 
 
 def exchange(values, axis):
     return lax.all_to_all(values, axis, 0, 0, tiled=True)
+
+
+def near_core(values):
+    return pltpu.with_memory_space_constraint(values, pltpu.VMEM)
+
+
+def in_place(values):
+    return pltpu.with_memory_space_constraint(values, pltpu.HBM)
 
 
 def body(vectors, kernel_hat, noise_prec, stencil_coefficients_raw, offsets, amplitude, cheb_coef):
@@ -385,6 +392,7 @@
     padded_time = 512
     full_high, full_low, to_time, to_frequency, fine = tables(length, block, blocks, padded_time)
     f32, bf16 = jnp.float32, jnp.bfloat16
+    to_time, to_frequency, fine = (near_core(jnp.asarray(table)) for table in (to_time, to_frequency, fine))
     grid_scratch = [
         pltpu.VMEM((all_points // LANES, SPAN, SPAN), bf16),
         pltpu.VMEM((all_points, LANES), f32),
@@ -395,57 +403,64 @@
     source = call(
         source_kernel,
         "source",
-        (blocks, points, LANES),
+        [((blocks, points, LANES), f32)],
         [VMEM] * 6,
         [pltpu.VMEM((count * points, padded_time), f32), pltpu.VMEM((LANES, LANES), f32)],
-    )(vectors, stencil_coefficients_raw.T, offsets.T, amplitude.reshape(1, points), full_high, full_low)
-    spectrum = exchange(source, "pts").reshape(all_points, LANES)
-    data = call(
+    )(
+        *map(
+            in_place,
+            (
+                vectors,
+                stencil_coefficients_raw.T,
+                offsets.T,
+                amplitude.reshape(1, points),
+                jnp.asarray(full_high),
+                jnp.asarray(full_low),
+            ),
+        )
+    )
+    spectrum = near_core(exchange(source, "pts").reshape(all_points, LANES))
+    data, kernel_high, kernel_low = call(
         partial(forward_kernel, near),
         "forward",
-        (sensors, LANES),
-        [VMEM, SMEM, ANY],
+        [((sensors, LANES), f32), (kernel_hat.shape, bf16), (kernel_hat.shape, bf16)],
+        [VMEM, SMEM, HBM],
         grid_scratch
         + [
             pltpu.VMEM((all_points, SPAN), bf16),
             pltpu.VMEM(kernel_hat.shape, f32),
             pltpu.SemaphoreType.DMA((block // 2,)),
         ],
-    )(spectrum, cheb_coef, kernel_hat)
-    data = exchange(data.reshape(blocks, sensors // blocks, LANES), "pts").reshape(sensors, LANES)
+    )(spectrum, cheb_coef, in_place(kernel_hat))
+    data = near_core(exchange(data.reshape(blocks, sensors // blocks, LANES), "pts").reshape(sensors, LANES))
     back = call(
         partial(sensor_kernel, block, length),
         "sensor",
-        (sensors, LANES),
+        [((sensors, LANES), f32)],
         [VMEM, SMEM, VMEM, VMEM, VMEM],
         [pltpu.VMEM((2 * SPAN, 2 * padded_time), bf16)],
     )(data, noise_prec, to_time, to_frequency, fine)
-    back = exchange(back.reshape(blocks, sensors // blocks, LANES), "pts").reshape(sensors, LANES)
+    back = near_core(exchange(back.reshape(blocks, sensors // blocks, LANES), "pts").reshape(sensors, LANES))
     partial_sums = call(
         partial(adjoint_kernel, near),
         "adjoint",
-        (groups, all_points // groups, LANES),
-        [VMEM, VMEM, SMEM, ANY],
+        [((groups, all_points // groups, LANES), f32)],
+        [VMEM, VMEM, SMEM, VMEM, VMEM],
         grid_scratch
-        + [
-            pltpu.VMEM((all_points, LANES), f32),
-            pltpu.VMEM(kernel_hat.shape, f32),
-            pltpu.VMEM((SLOTS, all_points + 2 * LANES), f32),
-            pltpu.SemaphoreType.DMA((all_points // SPAN,)),
-        ],
-    )(back, spectrum, cheb_coef, kernel_hat)
+        + [pltpu.VMEM((all_points, LANES), f32), pltpu.VMEM((SLOTS, all_points + 2 * LANES), f32)],
+    )(back, spectrum, cheb_coef, near_core(kernel_high), near_core(kernel_low))
     summed = jnp.sum(exchange(partial_sums, "sens"), axis=0)
     share = points // groups
-    moved = exchange(summed.reshape(blocks, share, LANES), "pts").reshape(blocks * share, LANES)
+    moved = near_core(exchange(summed.reshape(blocks, share, LANES), "pts").reshape(blocks * share, LANES))
     gradient = call(
         partial(gradient_kernel, block, length),
         "gradient",
-        (groups, share * count * padded_time // LANES, LANES),
+        [((groups, share * count * padded_time // LANES, LANES), f32)],
         [VMEM, VMEM, VMEM],
         [pltpu.VMEM((share * count * padded_time // LANES, LANES), f32)],
     )(moved, to_time, fine)
-    gathered = exchange(gradient, "sens")
-    return call(final_kernel, "final", (count, points, length), [VMEM, VMEM])(gathered, vectors)
+    gathered = near_core(exchange(gradient, "sens"))
+    return call(final_kernel, "final", [((count, points, length), f32)], [VMEM, VMEM], fast=False)(gathered, vectors)
 
 
 def solution(mesh):

time: 127 us -> 113 us (0.89)
  Pallas kernels: 28.4 us -> 18.9 us
  blocking collectives: 98 us -> 93.3 us
    pallas_call x6, Pallas kernels: 28.4 us -> 18.9 us  [the longest x1 9.73 us: body(): call(partial(forward_kernel, near), 'forward', [((sensors, LANES), f32),...]
    all_to_all x6, blocking collectives: 98 us -> 93.3 us  [exchange(): return lax.all_to_all(values, axis, 0, 0, tiled=True)]
where the time goes in v1:
time: 113 us; the launch traced here: 112 us
  blocking collectives  93.3 us (83%)
  Pallas kernels  18.9 us (17%)
    all_to_all x6, blocking collectives, exchange(): return lax.all_to_all(values, axis, 0, 0, tiled=True)  93.3 us
    pallas_call x1, Pallas kernels, body(): call(partial(forward_kernel, near), 'forward', [((sensors, LANES), f32),...  9.73 us
    pallas_call x1, Pallas kernels, body(): call(partial(adjoint_kernel, near), 'adjoint', [((groups, all_points // g...  3.92 us
    pallas_call x1, Pallas kernels, body(): call(source_kernel, 'source', [((blocks, points, LANES), f32)], [VMEM] *...  2.53 us

profile of v1, /device:TPU:1, one launch (start us, length us, event | category | flops | bytes accessed | tf_op | source)
XLA Modules:
  0.0 112.3 jit_solution(15631500376372544854)
XLA Ops:
  0.0 0.0 copy-start.4
  0.0 2.5 %source.1 = f32[32,32,128]{2,1,0:T(8,128)S(1)} custom-call(f32[4,32,420]{2,1,0:T(8,128)} %vectors.3, f32[6,32]{1,0:T(8,128)} %bitcast.18, s32[6,32]{1,0:T(8,128)} %bitcast.19, f32[1,32]{1,0:T(1,128)} %bitcast.20, bf16[512,1024]{1,0:T(8,128)(2,1)} %constant.15.clone.full_high, bf16[512,1024]{1,0:T(8,128)(2,1)} %constant.16.clone.full_low), custom_call_target="tpu_custom_call" | custom-call | tf_op jit(solution)/shard_map/source/pallas_call | solution.py:403
  2.5 29.2 %all_to_all.30 = f32[32,32,128]{2,1,0:T(8,128)S(1)} all-to-all(f32[32,32,128]{2,1,0:T(8,128)S(1)} %source.1), channel_id=1, replica_groups=mesh['sens'=8,'pts'=32] {'pts'}, dimensions={0} | all-to-all | bytes 1048576 | tf_op jit(solution)/shard_map/all_to_all | solution.py:373
  31.8 0.0 copy-done.4
  31.8 0.0 copy-start.1
  31.8 0.0 copy-start.2
  31.8 0.0 copy-start.3
  31.8 0.0 copy-start.5
  31.8 9.7 %forward.1 = (f32[64,128]{1,0:T(8,128)S(1)}, bf16[2,14,64,1024]{3,2,1,0:T(8,128)(2,1)S(1)}, bf16[2,14,64,1024]{3,2,1,0:T(8,128)(2,1)S(1)}) custom-call(f32[1024,128]{1,0:T(8,128)S(1)} %bitcast.10, f32[5]{0:T(128)S(1)} %copy-done.4, f32[2,14,64,1024]{3,2,1,0:T(8,128)} %kernel.1), custom_call_target="tpu_custom_call" | custom-call | tf_op jit(solution)/shard_map/forward/pallas_call | solution.py:423
  41.5 15.2 %all_to_all.31 = f32[32,2,128]{2,1,0:T(2,128)S(1)} all-to-all(f32[32,2,128]{2,1,0:T(2,128)S(1)} %bitcast.16), channel_id=1, replica_groups=mesh['sens'=8,'pts'=32] {'pts'}, dimensions={0} | all-to-all | bytes 65536 | tf_op jit(solution)/shard_map/all_to_all | solution.py:373
  56.8 0.0 copy-done.1
  56.8 0.0 copy-done.2
  56.8 0.0 copy-done.3
  56.8 0.0 copy-done.5
  56.8 1.4 %sensor.1 = f32[64,128]{1,0:T(8,128)S(1)} custom-call(f32[64,128]{1,0:T(8,128)S(1)} %bitcast.14, f32[2]{0:T(128)S(1)} %copy-done.5, bf16[128,1024]{1,0:T(8,128)(2,1)S(1)} %copy-done.1, bf16[1024,64]{1,0:T(8,128)(2,1)S(1)} %copy-done.3, f32[2,32,512]{2,1,0:T(8,128)S(1)} %copy-done.2), custom_call_target="tpu_custom_call" | custom-call | tf_op jit(solution)/shard_map/sensor/pallas_call | solution.py:436
  58.2 12.8 %all_to_all.32 = f32[32,2,128]{2,1,0:T(2,128)S(1)} all-to-all(f32[32,2,128]{2,1,0:T(2,128)S(1)} %bitcast.15), channel_id=1, replica_groups=mesh['sens'=8,'pts'=32] {'pts'}, dimensions={0} | all-to-all | bytes 65536 | tf_op jit(solution)/shard_map/all_to_all | solution.py:373
  70.9 0.0 copy-start
  70.9 3.9 %adjoint.1 = f32[8,128,128]{2,1,0:T(8,128)S(1)} custom-call(f32[64,128]{1,0:T(8,128)S(1)} %bitcast.13, f32[1024,128]{1,0:T(8,128)S(1)} %bitcast.11, f32[5]{0:T(128)S(1)} %copy-done.4, bf16[2,14,64,1024]{3,2,1,0:T(8,128)(2,1)S(1)} %get-tuple-element.9.highs, bf16[2,14,64,1024]{3,2,1,0:T(8,128)(2,1)S(1)} %get-tuple-element.10.lows), custom_call_target="tpu_custom_call" | custom-call | tf_op jit(solution)/shard_map/adjoint/pallas_call | solution.py:444
  74.8 12.8 %all_to_all.33 = f32[8,128,128]{2,1,0:T(8,128)S(1)} all-to-all(f32[8,128,128]{2,1,0:T(8,128)S(1)} %adjoint.1), channel_id=1, replica_groups=mesh['sens'=8,'pts'=32] {'sens'}, dimensions={0} | all-to-all | bytes 1048576 | tf_op jit(solution)/shard_map/all_to_all | solution.py:373
  87.7 14.7 %all_to_all.34 = f32[32,4,128]{2,1,0:T(4,128)S(1)} all-to-all(f32[32,4,128]{2,1,0:T(4,128)S(1)} %bitcast.17), channel_id=1, replica_groups=mesh['sens'=8,'pts'=32] {'pts'}, dimensions={0} | all-to-all | bytes 131072 | tf_op jit(solution)/shard_map/all_to_all | solution.py:373
  102.4 0.6 gradient.1
  103.0 8.6 %all_to_all.35.received = f32[8,64,128]{2,1,0:T(8,128)S(1)} all-to-all(f32[8,64,128]{2,1,0:T(8,128)S(1)} %gradient.1), channel_id=1, replica_groups=mesh['sens'=8,'pts'=32] {'sens'}, dimensions={0} | all-to-all | bytes 524288 | tf_op jit(solution)/shard_map/all_to_all | solution.py:373
  111.6 0.0 copy-done
  111.6 0.8 final.1
  (1 shorter events, 0.0 us)
Async XLA Ops:
  0.0 31.8 %copy-start.4 = (f32[5]{0:T(128)S(1)}, f32[5]{0:T(128)}, u32[]{:S(2)}) copy-start(f32[5]{0:T(128)} %coef.3) | copy-start | bytes 64
  31.8 25.0 %copy-start.1 = (bf16[128,1024]{1,0:T(8,128)(2,1)S(1)}, bf16[128,1024]{1,0:T(8,128)(2,1)}, u32[]{:S(2)}) copy-start(bf16[128,1024]{1,0:T(8,128)(2,1)} %constant.12.clone.to_time) | copy-start | bytes 786436
  31.8 25.0 %copy-start.2 = (f32[2,32,512]{2,1,0:T(8,128)S(1)}, f32[2,32,512]{2,1,0:T(8,128)}, u32[]{:S(2)}) copy-start(f32[2,32,512]{2,1,0:T(8,128)} %constant.14.clone.fine) | copy-start | bytes 393220
  31.8 25.0 %copy-start.3 = (bf16[1024,64]{1,0:T(8,128)(2,1)S(1)}, bf16[1024,64]{1,0:T(8,128)(2,1)}, u32[]{:S(2)}) copy-start(bf16[1024,64]{1,0:T(8,128)(2,1)} %constant.13.clone.to_frequency) | copy-start | bytes 393220
  31.8 25.0 %copy-start.5 = (f32[2]{0:T(128)S(1)}, f32[2]{0:T(128)}, u32[]{:S(2)}) copy-start(f32[2]{0:T(128)} %noise.1) | copy-start | bytes 28
  70.9 40.7 %copy-start = (f32[4,32,420]{2,1,0:T(8,128)S(1)}, f32[4,32,420]{2,1,0:T(8,128)}, u32[]{:S(2)}) copy-start(f32[4,32,420]{2,1,0:T(8,128)} %vectors.3) | copy-start | bytes 645124

commit v2 on v1

--- a/solution.py
+++ b/solution.py
@@ -106,50 +106,30 @@
                 out[start // 32 + tile * 4 + e] = block
 
 
-def chebyshev(load, store, band, coef, previous, current, total, state):
-    points = total.shape[0]
-    rows = LANES
-    blocks = points // rows
-    edge = jnp.zeros((REACH, SPAN), jnp.bfloat16)
-    for parity in range(2):
-        state[parity, :REACH] = edge
-        state[parity, REACH + points :] = edge
-
-    def put(parity, b, values):
-        high, low = halves(values)
-        state[parity, REACH + b * rows : REACH + (b + 1) * rows, :LANES] = high
-        state[parity, REACH + b * rows : REACH + (b + 1) * rows, LANES:] = low
+def chebyshev(blocks, apply, put, load, store, coef, previous, current, total):
+    def at(b):
+        return slice(b * LANES, (b + 1) * LANES)
 
     for b in range(blocks):
-        at = slice(b * rows, (b + 1) * rows)
         values = load(b)
-        previous[at] = values
-        total[at] = coef[0] * values
+        previous[at(b)] = values
+        total[at(b)] = coef[0] * values
         put(0, b, values)
     degree = coef.shape[0] - 1
     for j in range(1, degree + 1):
+        moved = apply((j - 1) % 2)
         for b in range(blocks):
-            at = slice(b * rows, (b + 1) * rows)
-            product = dot(band[b], state[(j - 1) % 2, b * rows : b * rows + SPAN])
-            moved = product[:rows, :LANES] + product[:rows, LANES:] + product[rows:, :LANES]
-            if j == 1:
-                values = moved
-            else:
-                values = 2.0 * moved - previous[at]
+            values = moved(b)
+            if j > 1:
+                values = 2.0 * values - previous[at(b)]
                 if j < degree:
-                    previous[at] = current[at]
+                    previous[at(b)] = current[at(b)]
             if j < degree:
-                current[at] = values
-                total[at] = total[at] + coef[j] * values
+                current[at(b)] = values
+                total[at(b)] = total[at(b)] + coef[j] * values
                 put(j % 2, b, values)
             else:
-                store(b, total[at] + coef[j] * values)
-
-
-def put_band(band, b, matrix):
-    high, low = halves(matrix)
-    band[b, :LANES] = high
-    band[b, LANES:] = low
+                store(b, total[at(b)] + coef[j] * values)
 
 
 def item(table, index):
@@ -169,24 +149,51 @@
 
 
 def forward_kernel(
-    near, received, coef, kernel, out, highs, lows, band, previous, current, total, state, ready, held, sems
+    near, received, coef, kernel, out, highs, lows, scatter, gather, previous, current, total, state, ready, held, sems
 ):
     pairs = sems.shape[0]
     copies = []
     for g in range(pairs):
-        copy = pltpu.make_async_copy(kernel.at[:, pl.ds(2 * g, 2)], held.at[:, pl.ds(2 * g, 2)], sems.at[g])
+        copies.append(
+            pltpu.make_async_copy(kernel.at[:, pl.ds(2 * g, 2)], held.at[:, pl.ds(2 * g, 2)], sems.at[g])
+        )
+    early = (pairs + 1) // 2
+    for copy in copies[:early]:
         copy.start()
-        copies.append(copy)
     points = total.shape[0]
-    column = iota((LANES, SPAN), 1).astype(jnp.float32)
-    row = iota((LANES, 1), 0).astype(jnp.float32)
-    for b in range(points // LANES):
-        table = received[b * LANES : (b + 1) * LANES]
-        matrix = jnp.zeros((LANES, SPAN), jnp.float32)
+    blocks = points // LANES
+    half = REACH // 2
+    row = iota((SPAN - REACH, LANES), 0).astype(jnp.float32)
+    column = iota((1, LANES), 1).astype(jnp.float32) + float(half)
+    edge = jnp.zeros((half, LANES), jnp.float32)
+    for b in range(blocks):
+        turned = received[b * LANES : (b + 1) * LANES].T
+        matrix = jnp.zeros((SPAN - REACH, LANES), jnp.float32)
         for k in range(near):
-            target = item(table, near + k) + (row + float(REACH))
-            matrix = matrix + jnp.where(column == target, item(table, k), 0.0)
-        put_band(band, b, matrix)
+            lane, shift = spare_lane(k), spare_lane(near + k)
+            target = turned[shift : shift + 1] + column
+            matrix = matrix + jnp.where(row == target, turned[lane : lane + 1], 0.0)
+        high, low = halves(jnp.concatenate([edge, matrix, edge], axis=0))
+        both = jnp.concatenate([high, low], axis=1)
+        scatter[b] = both
+        gather[b] = both.T
+    border = jnp.zeros((REACH, SPAN), jnp.bfloat16)
+    for parity in range(2):
+        state[parity, :REACH] = border
+        state[parity, REACH + points :] = border
+
+    def put(parity, b, values):
+        high, low = halves(values)
+        at = slice(REACH + b * LANES, REACH + (b + 1) * LANES)
+        state[parity, at, :LANES] = high
+        state[parity, at, LANES:] = low
+
+    def apply(parity):
+        def moved(b):
+            product = dot(gather[b], state[parity, b * LANES : b * LANES + SPAN])
+            return product[:LANES, :LANES] + product[:LANES, LANES:] + product[LANES:, :LANES]
+
+        return moved
 
     def load(b):
         return received[b * LANES : (b + 1) * LANES]
@@ -197,13 +204,19 @@
         ready[at, :LANES] = high
         ready[at, LANES:] = low
 
-    chebyshev(load, store, band, coef, previous, current, total, state)
+    chebyshev(blocks, apply, put, load, store, coef, previous, current, total)
     sensors = out.shape[0]
     of_lane = lane_frequency((sensors, LANES))
     direct = jnp.zeros((sensors, LANES), jnp.float32)
     crossed = jnp.zeros((sensors, LANES), jnp.float32)
+    for copy in copies[:early]:
+        copy.wait()
+    for copy in copies[early:]:
+        copy.start()
     for g in range(pairs):
-        copies[g].wait()
+        if g == early:
+            for copy in copies[early:]:
+                copy.wait()
         parts = []
         for f in (2 * g, 2 * g + 1):
             for c in range(2):
@@ -273,42 +286,67 @@
         out[pl.ds(n, blocks, stride=2), :] = result.T
 
 
-def adjoint_kernel(near, received, table, coef, highs, lows, out, band, previous, current, total, state, flat, stencil):
+def adjoint_kernel(near, received, table, coef, highs, lows, scatter, out, previous, current, total, state, flat, grid):
+    grid[...] = jnp.zeros_like(grid)
     chunks = highs.shape[3] // SPAN
     frequencies = highs.shape[1]
     points = total.shape[0]
     blocks = points // LANES
-    stencil[...] = jnp.zeros_like(stencil)
-    for b in range(blocks):
-        turned = table[b * LANES : (b + 1) * LANES].T
-        for m in range(2 * near):
-            lane = spare_lane(m)
-            stencil[m : m + 1, (b + 1) * LANES : (b + 2) * LANES] = turned[lane : lane + 1]
-    row = iota((LANES, SPAN), 0).astype(jnp.float32)
-    column = iota((1, SPAN), 1).astype(jnp.float32) - float(REACH)
-    for b in range(blocks):
-        window = pltpu.roll(stencil[:, b * LANES : (b + 3) * LANES], 3 * LANES - REACH, 1)[:, :SPAN]
-        matrix = jnp.zeros((LANES, SPAN), jnp.float32)
-        for k in range(near):
-            target = window[near + k : near + k + 1] + column
-            matrix = matrix + jnp.where(row == target, window[k : k + 1], 0.0)
-        put_band(band, b, matrix)
-    sensors = received.shape[0]
     values = received[...]
     real, following, leading = swapped(values)
     turned = jnp.concatenate([values, jnp.where(real, following, -leading)], axis=0).T
     high, low = halves(turned)
-    both = jnp.concatenate([high, low], axis=0)
-    of_row = ((iota((2 * LANES, LANES), 0) % 32) // 2)
-    spread = jnp.concatenate(
-        [jnp.where(of_row == f, both, jnp.zeros_like(both)) for f in range(frequencies)], axis=1
-    )
+    pairs = frequencies // 2
+    near_half = (iota((16, LANES), 0) % 4) // 2 == 0
+    left = []
+    for g in range(pairs):
+        rows = []
+        for part in (turned, turned - high.astype(jnp.float32)):
+            picked = jnp.concatenate([part[32 * v + 4 * g : 32 * v + 4 * g + 4] for v in range(4)], axis=0)
+            rows.append(
+                jnp.concatenate([jnp.where(near_half, picked, 0.0), jnp.where(near_half, 0.0, picked)], axis=1)
+            )
+        left.append(jnp.concatenate(rows, axis=0).astype(jnp.bfloat16))
     for n in range(chunks):
         at = slice(n * SPAN, (n + 1) * SPAN)
-        order = [(c, f) for f in range(frequencies) for c in range(2)]
-        first = dot(spread, jnp.concatenate([highs[c, f, :, at] for c, f in order], axis=0))
-        second = dot(spread[:LANES], jnp.concatenate([lows[c, f, :, at] for c, f in order], axis=0))
-        flat[n * SPAN : (n + 1) * SPAN] = (first[:LANES] + first[LANES:] + second).T
+        for g in range(pairs):
+            order = [(c, f) for f in (2 * g, 2 * g + 1) for c in range(2)]
+            first = dot(left[g], jnp.concatenate([highs[c, f, :, at] for c, f in order], axis=0))
+            second = dot(left[g][:16], jnp.concatenate([lows[c, f, :, at] for c, f in order], axis=0))
+            result = first[:16] + first[16:] + second
+            for v in range(4):
+                grid[32 * v + 4 * g : 32 * v + 4 * g + 4] = result[4 * v : 4 * v + 4]
+        flat[n * SPAN : (n + 1) * SPAN] = grid[...].T
+
+    blank = jnp.zeros((LANES, LANES), jnp.bfloat16)
+    for parity in range(2):
+        for b in range(blocks):
+            state[parity, b, LANES:, LANES:] = blank
+
+    def put(parity, b, values):
+        high, low = halves(values)
+        state[parity, b, :LANES, :LANES] = high
+        state[parity, b, :LANES, LANES:] = low
+        state[parity, b, LANES:, :LANES] = high
+
+    half = REACH // 2
+
+    def apply(parity):
+        spreads = []
+        for b in range(blocks):
+            product = dot(scatter[b], state[parity, b])
+            spreads.append(product[:, :LANES] + product[:, LANES:])
+
+        def moved(b):
+            middle = spreads[b][REACH : REACH + LANES]
+            first, last = middle[:half], middle[LANES - half :]
+            if b > 0:
+                first = first + spreads[b - 1][REACH + LANES : REACH + LANES + half]
+            if b < blocks - 1:
+                last = last + spreads[b + 1][half:REACH]
+            return jnp.concatenate([first, middle[half : LANES - half], last], axis=0)
+
+        return moved
 
     def load(b):
         at = slice(b * LANES, (b + 1) * LANES)
@@ -320,7 +358,7 @@
                 at = 16 * b + 4 * i
                 out[j, at : at + 4] = values[32 * i + 4 * j : 32 * i + 4 * j + 4]
 
-    chebyshev(load, store, band, coef, previous, current, total, state)
+    chebyshev(blocks, apply, put, load, store, coef, previous, current, total)
 
 
 def gradient_kernel(block, length, received, to_time, fine, out, once):
@@ -393,12 +431,11 @@
     full_high, full_low, to_time, to_frequency, fine = tables(length, block, blocks, padded_time)
     f32, bf16 = jnp.float32, jnp.bfloat16
     to_time, to_frequency, fine = (near_core(jnp.asarray(table)) for table in (to_time, to_frequency, fine))
+    bands = (all_points // LANES, SPAN, SPAN)
     grid_scratch = [
-        pltpu.VMEM((all_points // LANES, SPAN, SPAN), bf16),
         pltpu.VMEM((all_points, LANES), f32),
         pltpu.VMEM((all_points, LANES), f32),
         pltpu.VMEM((all_points, LANES), f32),
-        pltpu.VMEM((2, all_points + 2 * REACH, SPAN), bf16),
     ]
     source = call(
         source_kernel,
@@ -420,13 +457,15 @@
         )
     )
     spectrum = near_core(exchange(source, "pts").reshape(all_points, LANES))
-    data, kernel_high, kernel_low = call(
+    data, kernel_high, kernel_low, scatter = call(
         partial(forward_kernel, near),
         "forward",
-        [((sensors, LANES), f32), (kernel_hat.shape, bf16), (kernel_hat.shape, bf16)],
+        [((sensors, LANES), f32), (kernel_hat.shape, bf16), (kernel_hat.shape, bf16), (bands, bf16)],
         [VMEM, SMEM, HBM],
-        grid_scratch
+        [pltpu.VMEM(bands, bf16)]
+        + grid_scratch
         + [
+            pltpu.VMEM((2, all_points + 2 * REACH, SPAN), bf16),
             pltpu.VMEM((all_points, SPAN), bf16),
             pltpu.VMEM(kernel_hat.shape, f32),
             pltpu.SemaphoreType.DMA((block // 2,)),
@@ -445,10 +484,9 @@
         partial(adjoint_kernel, near),
         "adjoint",
         [((groups, all_points // groups, LANES), f32)],
-        [VMEM, VMEM, SMEM, VMEM, VMEM],
-        grid_scratch
-        + [pltpu.VMEM((all_points, LANES), f32), pltpu.VMEM((SLOTS, all_points + 2 * LANES), f32)],
-    )(back, spectrum, cheb_coef, near_core(kernel_high), near_core(kernel_low))
+        [VMEM, VMEM, SMEM, VMEM, VMEM, VMEM],
+        grid_scratch + [pltpu.VMEM((2,) + bands, bf16), pltpu.VMEM((all_points, LANES), f32), pltpu.VMEM((LANES, SPAN), f32)],
+    )(back, spectrum, cheb_coef, near_core(kernel_high), near_core(kernel_low), near_core(scatter))
     summed = jnp.sum(exchange(partial_sums, "sens"), axis=0)
     share = points // groups
     moved = near_core(exchange(summed.reshape(blocks, share, LANES), "pts").reshape(blocks * share, LANES))

time: 113 us -> 110 us (0.973)
  Pallas kernels: 18.9 us -> 15.8 us
    pallas_call x1, Pallas kernels: 9.73 us -> 7.4 us  [body(): call(partial(forward_kernel, near), 'forward', [((sensors, LANES), f32),...]
where the time goes in v2:
time: 110 us; the launch traced here: 109 us
  blocking collectives  93.3 us (85%)
  Pallas kernels  15.8 us (14%)
    all_to_all x6, blocking collectives, exchange(): return lax.all_to_all(values, axis, 0, 0, tiled=True)  93.3 us
    pallas_call x1, Pallas kernels, body(): call(partial(forward_kernel, near), 'forward', [((sensors, LANES), f32),...  7.4 us
    pallas_call x1, Pallas kernels, body(): call(partial(adjoint_kernel, near), 'adjoint', [((groups, all_points // g...  3.19 us
    pallas_call x1, Pallas kernels, body(): call(source_kernel, 'source', [((blocks, points, LANES), f32)], [VMEM] *...  2.53 us

profile of v2, /device:TPU:1, one launch (start us, length us, event | category | flops | bytes accessed | tf_op | source)
XLA Modules:
  0.0 109.3 jit_solution(8802398678572821700)
XLA Ops:
  0.0 0.0 copy-start.4
  0.0 2.5 %source.1 = f32[32,32,128]{2,1,0:T(8,128)S(1)} custom-call(f32[4,32,420]{2,1,0:T(8,128)} %vectors.3, f32[6,32]{1,0:T(8,128)} %bitcast.18, s32[6,32]{1,0:T(8,128)} %bitcast.19, f32[1,32]{1,0:T(1,128)} %bitcast.20, bf16[512,1024]{1,0:T(8,128)(2,1)} %constant.15.clone.full_high, bf16[512,1024]{1,0:T(8,128)(2,1)} %constant.16.clone.full_low), custom_call_target="tpu_custom_call" | custom-call | tf_op jit(solution)/shard_map/source/pallas_call | solution.py:440
  2.5 29.2 %all_to_all.30 = f32[32,32,128]{2,1,0:T(8,128)S(1)} all-to-all(f32[32,32,128]{2,1,0:T(8,128)S(1)} %source.1), channel_id=1, replica_groups=mesh['sens'=8,'pts'=32] {'pts'}, dimensions={0} | all-to-all | bytes 1048576 | tf_op jit(solution)/shard_map/all_to_all | solution.py:411
  31.8 0.0 copy-done.4
  31.8 0.0 copy-start.1
  31.8 0.0 copy-start.2
  31.8 0.0 copy-start.3
  31.8 0.0 copy-start.5
  31.8 7.4 %forward.1 = (f32[64,128]{1,0:T(8,128)S(1)}, bf16[2,14,64,1024]{3,2,1,0:T(8,128)(2,1)S(1)}, bf16[2,14,64,1024]{3,2,1,0:T(8,128)(2,1)S(1)}, bf16[8,256,256]{2,1,0:T(8,128)(2,1)S(1)}) custom-call(f32[1024,128]{1,0:T(8,128)S(1)} %bitcast.10, f32[5]{0:T(128)S(1)} %copy-done.4, f32[2,14,64,1024]{3,2,1,0:T(8,128)} %kernel.1), custom_call_target="tpu_custom_call" | custom-call | tf_op jit(solution)/shard_map/forward/pallas_call | solution.py:460
  39.2 15.2 %all_to_all.31 = f32[32,2,128]{2,1,0:T(2,128)S(1)} all-to-all(f32[32,2,128]{2,1,0:T(2,128)S(1)} %bitcast.16), channel_id=1, replica_groups=mesh['sens'=8,'pts'=32] {'pts'}, dimensions={0} | all-to-all | bytes 65536 | tf_op jit(solution)/shard_map/all_to_all | solution.py:411
  54.4 0.0 copy-done.1
  54.4 0.0 copy-done.2
  54.4 0.0 copy-done.3
  54.4 0.0 copy-done.5
  54.5 1.4 %sensor.1 = f32[64,128]{1,0:T(8,128)S(1)} custom-call(f32[64,128]{1,0:T(8,128)S(1)} %bitcast.14, f32[2]{0:T(128)S(1)} %copy-done.5, bf16[128,1024]{1,0:T(8,128)(2,1)S(1)} %copy-done.1, bf16[1024,64]{1,0:T(8,128)(2,1)S(1)} %copy-done.3, f32[2,32,512]{2,1,0:T(8,128)S(1)} %copy-done.2), custom_call_target="tpu_custom_call" | custom-call | tf_op jit(solution)/shard_map/sensor/pallas_call | solution.py:475
  55.8 12.8 %all_to_all.32 = f32[32,2,128]{2,1,0:T(2,128)S(1)} all-to-all(f32[32,2,128]{2,1,0:T(2,128)S(1)} %bitcast.15), channel_id=1, replica_groups=mesh['sens'=8,'pts'=32] {'pts'}, dimensions={0} | all-to-all | bytes 65536 | tf_op jit(solution)/shard_map/all_to_all | solution.py:411
  68.6 0.0 copy-start
  68.6 3.2 %adjoint.1 = f32[8,128,128]{2,1,0:T(8,128)S(1)} custom-call(f32[64,128]{1,0:T(8,128)S(1)} %bitcast.13, f32[1024,128]{1,0:T(8,128)S(1)} %bitcast.11, f32[5]{0:T(128)S(1)} %copy-done.4, bf16[2,14,64,1024]{3,2,1,0:T(8,128)(2,1)S(1)} %get-tuple-element.10.highs, bf16[2,14,64,1024]{3,2,1,0:T(8,128)(2,1)S(1)} %get-tuple-element.11.lows, ...), custom_call_target="tpu_custom_call" | custom-call | tf_op jit(solution)/shard_map/adjoint/pallas_call | solution.py:483
  71.8 12.8 %all_to_all.33 = f32[8,128,128]{2,1,0:T(8,128)S(1)} all-to-all(f32[8,128,128]{2,1,0:T(8,128)S(1)} %adjoint.1), channel_id=1, replica_groups=mesh['sens'=8,'pts'=32] {'sens'}, dimensions={0} | all-to-all | bytes 1048576 | tf_op jit(solution)/shard_map/all_to_all | solution.py:411
  84.6 14.7 %all_to_all.34 = f32[32,4,128]{2,1,0:T(4,128)S(1)} all-to-all(f32[32,4,128]{2,1,0:T(4,128)S(1)} %bitcast.17), channel_id=1, replica_groups=mesh['sens'=8,'pts'=32] {'pts'}, dimensions={0} | all-to-all | bytes 131072 | tf_op jit(solution)/shard_map/all_to_all | solution.py:411
  99.3 0.6 gradient.1
  99.9 8.6 %all_to_all.35.received = f32[8,64,128]{2,1,0:T(8,128)S(1)} all-to-all(f32[8,64,128]{2,1,0:T(8,128)S(1)} %gradient.1), channel_id=1, replica_groups=mesh['sens'=8,'pts'=32] {'sens'}, dimensions={0} | all-to-all | bytes 524288 | tf_op jit(solution)/shard_map/all_to_all | solution.py:411
  108.5 0.0 copy-done
  108.5 0.8 final.1
  (1 shorter events, 0.0 us)
Async XLA Ops:
  0.0 31.8 %copy-start.4 = (f32[5]{0:T(128)S(1)}, f32[5]{0:T(128)}, u32[]{:S(2)}) copy-start(f32[5]{0:T(128)} %coef.3) | copy-start | bytes 64
  31.8 22.7 %copy-start.1 = (bf16[128,1024]{1,0:T(8,128)(2,1)S(1)}, bf16[128,1024]{1,0:T(8,128)(2,1)}, u32[]{:S(2)}) copy-start(bf16[128,1024]{1,0:T(8,128)(2,1)} %constant.12.clone.to_time) | copy-start | bytes 786436
  31.8 22.7 %copy-start.2 = (f32[2,32,512]{2,1,0:T(8,128)S(1)}, f32[2,32,512]{2,1,0:T(8,128)}, u32[]{:S(2)}) copy-start(f32[2,32,512]{2,1,0:T(8,128)} %constant.14.clone.fine) | copy-start | bytes 393220
  31.8 22.7 %copy-start.3 = (bf16[1024,64]{1,0:T(8,128)(2,1)S(1)}, bf16[1024,64]{1,0:T(8,128)(2,1)}, u32[]{:S(2)}) copy-start(bf16[1024,64]{1,0:T(8,128)(2,1)} %constant.13.clone.to_frequency) | copy-start | bytes 393220
  31.8 22.7 %copy-start.5 = (f32[2]{0:T(128)S(1)}, f32[2]{0:T(128)}, u32[]{:S(2)}) copy-start(f32[2]{0:T(128)} %noise.1) | copy-start | bytes 28
  68.6 39.9 %copy-start = (f32[4,32,420]{2,1,0:T(8,128)S(1)}, f32[4,32,420]{2,1,0:T(8,128)}, u32[]{:S(2)}) copy-start(f32[4,32,420]{2,1,0:T(8,128)} %vectors.3) | copy-start | bytes 645124

commit v3 on v2

--- a/solution.py
+++ b/solution.py
@@ -157,7 +157,7 @@
         copies.append(
             pltpu.make_async_copy(kernel.at[:, pl.ds(2 * g, 2)], held.at[:, pl.ds(2 * g, 2)], sems.at[g])
         )
-    early = (pairs + 1) // 2
+    early = pairs - 2
     for copy in copies[:early]:
         copy.start()
     points = total.shape[0]
@@ -366,9 +366,15 @@
     weight = frequency_weight(block, blocks, length)
 
     def each(n, v, values):
-        for tile in range(values.shape[1] // LANES):
+        for tile in range(values.shape[1] // LANES - 1):
             at = 16 * tile + 4 * v + n
             once[at : at + 1] = values[:, tile * LANES : (tile + 1) * LANES]
+        tail = values[:, values.shape[1] - LANES :]
+        at = 48 + 4 * (v // 2) + n
+        if v % 2:
+            once[at : at + 1] = once[at : at + 1] + pltpu.roll(tail, LANES // 2, 1)
+        else:
+            once[at : at + 1] = tail
 
     series(received, 4, blocks, weight, to_time, fine, each)
     for copy in range(out.shape[0]):
@@ -378,12 +384,17 @@
 def final_kernel(received, vectors, out):
     count, _, length = out.shape
     groups = received.shape[0]
-    for tile in range(received.shape[1] // 16):
-        lanes = min(LANES, length - tile * LANES)
-        at = slice(tile * LANES, tile * LANES + lanes)
+    for tile in range(3):
+        at = slice(tile * LANES, (tile + 1) * LANES)
         for v in range(count):
             rows = [received[j, 16 * tile + 4 * v : 16 * tile + 4 * v + 4] for j in range(groups)]
-            out[v, :, at] = vectors[v, :, at] + jnp.concatenate(rows, axis=0)[:, :lanes]
+            out[v, :, at] = vectors[v, :, at] + jnp.concatenate(rows, axis=0)
+    for v in range(count):
+        first = 48 + 4 * (v // 2)
+        rows = jnp.concatenate([received[j, first : first + 4] for j in range(groups)], axis=0)
+        if v % 2:
+            rows = pltpu.roll(rows, LANES // 2, 1)
+        out[v, :, 3 * LANES :] = vectors[v, :, 3 * LANES :] + rows[:, : length - 3 * LANES]
 
 
 VMEM = pl.BlockSpec(memory_space=pltpu.VMEM)
@@ -493,9 +504,9 @@
     gradient = call(
         partial(gradient_kernel, block, length),
         "gradient",
-        [((groups, share * count * padded_time // LANES, LANES), f32)],
+        [((groups, 56, LANES), f32)],
         [VMEM, VMEM, VMEM],
-        [pltpu.VMEM((share * count * padded_time // LANES, LANES), f32)],
+        [pltpu.VMEM((56, LANES), f32)],
     )(moved, to_time, fine)
     gathered = near_core(exchange(gradient, "sens"))
     return call(final_kernel, "final", [((count, points, length), f32)], [VMEM, VMEM], fast=False)(gathered, vectors)

time: 110 us -> 109 us (level)
  no operation moved by 1% of the time
where the time goes in v3:
time: 109 us
  blocking collectives  93.2 us (86%)
  Pallas kernels  15.4 us (14%)
    all_to_all x6, blocking collectives, exchange(): return lax.all_to_all(values, axis, 0, 0, tiled=True)  93.2 us
    pallas_call x1, Pallas kernels, body(): call(partial(forward_kernel, near), 'forward', [((sensors, LANES), f32),...  6.96 us
    pallas_call x1, Pallas kernels, body(): call(partial(adjoint_kernel, near), 'adjoint', [((groups, all_points // g...  3.19 us
    pallas_call x1, Pallas kernels, body(): call(source_kernel, 'source', [((blocks, points, LANES), f32)], [VMEM] *...  2.53 us

profile of v3, /device:TPU:1, one launch (start us, length us, event | category | flops | bytes accessed | tf_op | source)
XLA Modules:
  0.0 108.7 jit_solution(10600361414164671529)
XLA Ops:
  0.0 0.0 copy-start.4
  0.0 2.5 %source.1 = f32[32,32,128]{2,1,0:T(8,128)S(1)} custom-call(f32[4,32,420]{2,1,0:T(8,128)} %vectors.3, f32[6,32]{1,0:T(8,128)} %bitcast.18, s32[6,32]{1,0:T(8,128)} %bitcast.19, f32[1,32]{1,0:T(1,128)} %bitcast.20, bf16[512,1024]{1,0:T(8,128)(2,1)} %constant.15.clone.full_high, bf16[512,1024]{1,0:T(8,128)(2,1)} %constant.16.clone.full_low), custom_call_target="tpu_custom_call" | custom-call | tf_op jit(solution)/shard_map/source/pallas_call | solution.py:451
  2.5 29.2 %all_to_all.30 = f32[32,32,128]{2,1,0:T(8,128)S(1)} all-to-all(f32[32,32,128]{2,1,0:T(8,128)S(1)} %source.1), channel_id=1, replica_groups=mesh['sens'=8,'pts'=32] {'pts'}, dimensions={0} | all-to-all | bytes 1048576 | tf_op jit(solution)/shard_map/all_to_all | solution.py:422
  31.8 0.0 copy-done.4
  31.8 0.0 copy-start.1
  31.8 0.0 copy-start.2
  31.8 0.0 copy-start.3
  31.8 0.0 copy-start.5
  31.8 7.0 %forward.1 = (f32[64,128]{1,0:T(8,128)S(1)}, bf16[2,14,64,1024]{3,2,1,0:T(8,128)(2,1)S(1)}, bf16[2,14,64,1024]{3,2,1,0:T(8,128)(2,1)S(1)}, bf16[8,256,256]{2,1,0:T(8,128)(2,1)S(1)}) custom-call(f32[1024,128]{1,0:T(8,128)S(1)} %bitcast.10, f32[5]{0:T(128)S(1)} %copy-done.4, f32[2,14,64,1024]{3,2,1,0:T(8,128)} %kernel.1), custom_call_target="tpu_custom_call" | custom-call | tf_op jit(solution)/shard_map/forward/pallas_call | solution.py:471
  38.8 15.2 %all_to_all.31 = f32[32,2,128]{2,1,0:T(2,128)S(1)} all-to-all(f32[32,2,128]{2,1,0:T(2,128)S(1)} %bitcast.16), channel_id=1, replica_groups=mesh['sens'=8,'pts'=32] {'pts'}, dimensions={0} | all-to-all | bytes 65536 | tf_op jit(solution)/shard_map/all_to_all | solution.py:422
  54.0 0.0 copy-done.1
  54.0 0.0 copy-done.2
  54.0 0.0 copy-done.3
  54.0 0.0 copy-done.5
  54.0 1.4 %sensor.1 = f32[64,128]{1,0:T(8,128)S(1)} custom-call(f32[64,128]{1,0:T(8,128)S(1)} %bitcast.14, f32[2]{0:T(128)S(1)} %copy-done.5, bf16[128,1024]{1,0:T(8,128)(2,1)S(1)} %copy-done.1, bf16[1024,64]{1,0:T(8,128)(2,1)S(1)} %copy-done.3, f32[2,32,512]{2,1,0:T(8,128)S(1)} %copy-done.2), custom_call_target="tpu_custom_call" | custom-call | tf_op jit(solution)/shard_map/sensor/pallas_call | solution.py:486
  55.4 12.8 %all_to_all.32 = f32[32,2,128]{2,1,0:T(2,128)S(1)} all-to-all(f32[32,2,128]{2,1,0:T(2,128)S(1)} %bitcast.15), channel_id=1, replica_groups=mesh['sens'=8,'pts'=32] {'pts'}, dimensions={0} | all-to-all | bytes 65536 | tf_op jit(solution)/shard_map/all_to_all | solution.py:422
  68.1 0.0 copy-start
  68.1 3.2 %adjoint.1 = f32[8,128,128]{2,1,0:T(8,128)S(1)} custom-call(f32[64,128]{1,0:T(8,128)S(1)} %bitcast.13, f32[1024,128]{1,0:T(8,128)S(1)} %bitcast.11, f32[5]{0:T(128)S(1)} %copy-done.4, bf16[2,14,64,1024]{3,2,1,0:T(8,128)(2,1)S(1)} %get-tuple-element.10.highs, bf16[2,14,64,1024]{3,2,1,0:T(8,128)(2,1)S(1)} %get-tuple-element.11.lows, ...), custom_call_target="tpu_custom_call" | custom-call | tf_op jit(solution)/shard_map/adjoint/pallas_call | solution.py:494
  71.3 12.8 %all_to_all.33 = f32[8,128,128]{2,1,0:T(8,128)S(1)} all-to-all(f32[8,128,128]{2,1,0:T(8,128)S(1)} %adjoint.1), channel_id=1, replica_groups=mesh['sens'=8,'pts'=32] {'sens'}, dimensions={0} | all-to-all | bytes 1048576 | tf_op jit(solution)/shard_map/all_to_all | solution.py:422
  84.2 14.7 %all_to_all.34 = f32[32,4,128]{2,1,0:T(4,128)S(1)} all-to-all(f32[32,4,128]{2,1,0:T(4,128)S(1)} %bitcast.17), channel_id=1, replica_groups=mesh['sens'=8,'pts'=32] {'pts'}, dimensions={0} | all-to-all | bytes 131072 | tf_op jit(solution)/shard_map/all_to_all | solution.py:422
  98.9 0.6 gradient.1
  99.5 8.4 %all_to_all.35.received = f32[8,56,128]{2,1,0:T(8,128)S(1)} all-to-all(f32[8,56,128]{2,1,0:T(8,128)S(1)} %gradient.1), channel_id=1, replica_groups=mesh['sens'=8,'pts'=32] {'sens'}, dimensions={0} | all-to-all | bytes 458752 | tf_op jit(solution)/shard_map/all_to_all | solution.py:422
  108.0 0.0 copy-done
  108.0 0.8 final.1
  (1 shorter events, 0.0 us)
Async XLA Ops:
  0.0 31.8 %copy-start.4 = (f32[5]{0:T(128)S(1)}, f32[5]{0:T(128)}, u32[]{:S(2)}) copy-start(f32[5]{0:T(128)} %coef.3) | copy-start | bytes 64
  31.8 22.2 %copy-start.1 = (bf16[128,1024]{1,0:T(8,128)(2,1)S(1)}, bf16[128,1024]{1,0:T(8,128)(2,1)}, u32[]{:S(2)}) copy-start(bf16[128,1024]{1,0:T(8,128)(2,1)} %constant.12.clone.to_time) | copy-start | bytes 786436
  31.8 22.2 %copy-start.2 = (f32[2,32,512]{2,1,0:T(8,128)S(1)}, f32[2,32,512]{2,1,0:T(8,128)}, u32[]{:S(2)}) copy-start(f32[2,32,512]{2,1,0:T(8,128)} %constant.14.clone.fine) | copy-start | bytes 393220
  31.8 22.2 %copy-start.3 = (bf16[1024,64]{1,0:T(8,128)(2,1)S(1)}, bf16[1024,64]{1,0:T(8,128)(2,1)}, u32[]{:S(2)}) copy-start(bf16[1024,64]{1,0:T(8,128)(2,1)} %constant.13.clone.to_frequency) | copy-start | bytes 393220
  31.8 22.2 %copy-start.5 = (f32[2]{0:T(128)S(1)}, f32[2]{0:T(128)}, u32[]{:S(2)}) copy-start(f32[2]{0:T(128)} %noise.1) | copy-start | bytes 28
  68.1 39.8 %copy-start = (f32[4,32,420]{2,1,0:T(8,128)S(1)}, f32[4,32,420]{2,1,0:T(8,128)}, u32[]{:S(2)}) copy-start(f32[4,32,420]{2,1,0:T(8,128)} %vectors.3) | copy-start | bytes 645124

commit v4 on v3

--- a/solution.py
+++ b/solution.py
@@ -48,10 +48,11 @@
     fine[1, :block, 1, :length] = -np.cos(fine_angle)
     fine = fine.reshape(2, 2 * SLOTS, padded_time)
     full_angle = angle(np.arange(blocks * block)).reshape(blocks, block, length)
-    full = np.zeros((padded_time, blocks, SLOTS, 2))
+    rows = -(-length // 16) * 16
+    full = np.zeros((rows, blocks, SLOTS, 2))
     full[:length, :, :block, 0] = np.cos(full_angle).transpose(2, 0, 1)
     full[:length, :, :block, 1] = -np.sin(full_angle).transpose(2, 0, 1)
-    full = full.reshape(padded_time, blocks * 2 * SLOTS)
+    full = full.reshape(rows, blocks * 2 * SLOTS)
     coarse_high, coarse_low = host_halves(coarse)
     to_time = np.concatenate([coarse_high, coarse_high, coarse_low, coarse_low], axis=0)
     to_frequency = np.concatenate([coarse_high, coarse_low], axis=0).T.copy()
@@ -67,7 +68,7 @@
     return lax.broadcasted_iota(jnp.int32, shape, axis)
 
 
-def source_kernel(vectors, raw, offsets, amplitude, full_high, full_low, out, padded, items):
+def source_kernel(vectors, raw, offsets, amplitude, coef, full_high, full_low, out, padded, items):
     count, points, length = vectors.shape
     padded[...] = jnp.zeros_like(padded)
     for v in range(count):
@@ -83,9 +84,11 @@
         items[lane : lane + 1, :points] = shifts[k : k + 1]
     lane = spare_lane(2 * near)
     items[lane : lane + 1, :points] = amplitude[...]
+    lane = spare_lane(2 * near + 1)
+    items[lane : lane + 1, : coef.shape[1]] = coef[...]
     extra = items[...].T[:points]
     rows = count * points
-    high, low = halves(padded[...])
+    high, low = halves(padded[:, : full_high.shape[0]])
     both = jnp.concatenate([high, low], axis=0)
     group_of_lane = iota((points, LANES), 1) // 32
     width = SPAN
@@ -107,6 +110,8 @@
 
 
 def chebyshev(blocks, apply, put, load, store, coef, previous, current, total):
+    degree = len(coef) - 1
+
     def at(b):
         return slice(b * LANES, (b + 1) * LANES)
 
@@ -115,7 +120,6 @@
         previous[at(b)] = values
         total[at(b)] = coef[0] * values
         put(0, b, values)
-    degree = coef.shape[0] - 1
     for j in range(1, degree + 1):
         moved = apply((j - 1) % 2)
         for b in range(blocks):
@@ -137,6 +141,11 @@
     return table[:, lane : lane + 1]
 
 
+def coefficients(table, near, degree):
+    lane = spare_lane(2 * near + 1)
+    return [table[j : j + 1, lane : lane + 1] for j in range(degree + 1)]
+
+
 def lane_frequency(shape):
     return (iota(shape, 1) % 32) // 2
 
@@ -149,7 +158,7 @@
 
 
 def forward_kernel(
-    near, received, coef, kernel, out, highs, lows, scatter, gather, previous, current, total, state, ready, held, sems
+    near, degree, received, kernel, out, highs, lows, scatter, gather, previous, current, total, state, ready, held, sems
 ):
     pairs = sems.shape[0]
     copies = []
@@ -204,6 +213,7 @@
         ready[at, :LANES] = high
         ready[at, LANES:] = low
 
+    coef = coefficients(received, near, degree)
     chebyshev(blocks, apply, put, load, store, coef, previous, current, total)
     sensors = out.shape[0]
     of_lane = lane_frequency((sensors, LANES))
@@ -286,7 +296,7 @@
         out[pl.ds(n, blocks, stride=2), :] = result.T
 
 
-def adjoint_kernel(near, received, table, coef, highs, lows, scatter, out, previous, current, total, state, flat, grid):
+def adjoint_kernel(near, degree, received, table, highs, lows, scatter, out, previous, current, total, state, flat, grid):
     grid[...] = jnp.zeros_like(grid)
     chunks = highs.shape[3] // SPAN
     frequencies = highs.shape[1]
@@ -358,6 +368,7 @@
                 at = 16 * b + 4 * i
                 out[j, at : at + 4] = values[32 * i + 4 * j : 32 * i + 4 * j + 4]
 
+    coef = coefficients(table, near, degree)
     chebyshev(blocks, apply, put, load, store, coef, previous, current, total)
 
 
@@ -436,6 +447,7 @@
     count, points, length = vectors.shape
     _, block, sensors, all_points = kernel_hat.shape
     near = offsets.shape[1]
+    degree = cheb_coef.shape[0] - 1
     blocks = lax.axis_size("pts")
     groups = lax.axis_size("sens")
     padded_time = 512
@@ -452,7 +464,7 @@
         source_kernel,
         "source",
         [((blocks, points, LANES), f32)],
-        [VMEM] * 6,
+        [VMEM] * 7,
         [pltpu.VMEM((count * points, padded_time), f32), pltpu.VMEM((LANES, LANES), f32)],
     )(
         *map(
@@ -462,6 +474,7 @@
                 stencil_coefficients_raw.T,
                 offsets.T,
                 amplitude.reshape(1, points),
+                cheb_coef.reshape(1, -1),
                 jnp.asarray(full_high),
                 jnp.asarray(full_low),
             ),
@@ -469,10 +482,10 @@
     )
     spectrum = near_core(exchange(source, "pts").reshape(all_points, LANES))
     data, kernel_high, kernel_low, scatter = call(
-        partial(forward_kernel, near),
+        partial(forward_kernel, near, degree),
         "forward",
         [((sensors, LANES), f32), (kernel_hat.shape, bf16), (kernel_hat.shape, bf16), (bands, bf16)],
-        [VMEM, SMEM, HBM],
+        [VMEM, HBM],
         [pltpu.VMEM(bands, bf16)]
         + grid_scratch
         + [
@@ -481,7 +494,7 @@
             pltpu.VMEM(kernel_hat.shape, f32),
             pltpu.SemaphoreType.DMA((block // 2,)),
         ],
-    )(spectrum, cheb_coef, in_place(kernel_hat))
+    )(spectrum, in_place(kernel_hat))
     data = near_core(exchange(data.reshape(blocks, sensors // blocks, LANES), "pts").reshape(sensors, LANES))
     back = call(
         partial(sensor_kernel, block, length),
@@ -492,12 +505,12 @@
     )(data, noise_prec, to_time, to_frequency, fine)
     back = near_core(exchange(back.reshape(blocks, sensors // blocks, LANES), "pts").reshape(sensors, LANES))
     partial_sums = call(
-        partial(adjoint_kernel, near),
+        partial(adjoint_kernel, near, degree),
         "adjoint",
         [((groups, all_points // groups, LANES), f32)],
-        [VMEM, VMEM, SMEM, VMEM, VMEM, VMEM],
+        [VMEM, VMEM, VMEM, VMEM, VMEM],
         grid_scratch + [pltpu.VMEM((2,) + bands, bf16), pltpu.VMEM((all_points, LANES), f32), pltpu.VMEM((LANES, SPAN), f32)],
-    )(back, spectrum, cheb_coef, near_core(kernel_high), near_core(kernel_low), near_core(scatter))
+    )(back, spectrum, near_core(kernel_high), near_core(kernel_low), near_core(scatter))
     summed = jnp.sum(exchange(partial_sums, "sens"), axis=0)
     share = points // groups
     moved = near_core(exchange(summed.reshape(blocks, share, LANES), "pts").reshape(blocks * share, LANES))

time: 109 us -> 109 us (level)
  no operation moved by 1% of the time
where the time goes in v4:
time: 109 us; the launch traced here: 108 us
  blocking collectives  93.2 us (86%)
  Pallas kernels  15 us (14%)
    all_to_all x6, blocking collectives, exchange(): return lax.all_to_all(values, axis, 0, 0, tiled=True)  93.2 us
    pallas_call x1, Pallas kernels, body(): call(partial(forward_kernel, near, degree), 'forward', [((sensors, LANES)...  7.06 us
    pallas_call x1, Pallas kernels, body(): call(partial(adjoint_kernel, near, degree), 'adjoint', [((groups, all_poi...  2.73 us
    pallas_call x1, Pallas kernels, body(): call(source_kernel, 'source', [((blocks, points, LANES), f32)], [VMEM] *...  2.42 us

profile of v4, /device:TPU:1, one launch (start us, length us, event | category | flops | bytes accessed | tf_op | source)
XLA Modules:
  0.0 108.3 jit_solution(7321895966297419691)
XLA Ops:
  0.0 2.4 %source.1 = f32[32,32,128]{2,1,0:T(8,128)S(1)} custom-call(f32[4,32,420]{2,1,0:T(8,128)} %vectors.3, f32[6,32]{1,0:T(8,128)} %bitcast.19, s32[6,32]{1,0:T(8,128)} %bitcast.20, f32[1,32]{1,0:T(1,128)} %bitcast.21, f32[1,5]{1,0:T(1,128)} %bitcast.22, bf16[432,1024]{1,0:T(8,128)(2,1)} %constant.15.clone.full_high, bf16[432,1024]{1,0:T(8,128)(2,1)} %constant.16.clone.full_low), custom_call_target="tpu_custom_call" | custom-call | tf_op jit(solution)/shard_map/source/pallas_call | solution.py:463
  2.4 29.2 %all_to_all.30 = f32[32,32,128]{2,1,0:T(8,128)S(1)} all-to-all(f32[32,32,128]{2,1,0:T(8,128)S(1)} %source.1), channel_id=1, replica_groups=mesh['sens'=8,'pts'=32] {'pts'}, dimensions={0} | all-to-all | bytes 1048576 | tf_op jit(solution)/shard_map/all_to_all | solution.py:433
  31.6 0.0 copy-start.1
  31.6 0.0 copy-start.2
  31.7 0.0 copy-start.3
  31.7 0.0 copy-start.4
  31.7 7.1 %forward.1 = (f32[64,128]{1,0:T(8,128)S(1)}, bf16[2,14,64,1024]{3,2,1,0:T(8,128)(2,1)S(1)}, bf16[2,14,64,1024]{3,2,1,0:T(8,128)(2,1)S(1)}, bf16[8,256,256]{2,1,0:T(8,128)(2,1)S(1)}) custom-call(f32[1024,128]{1,0:T(8,128)S(1)} %bitcast.11, f32[2,14,64,1024]{3,2,1,0:T(8,128)} %kernel.1), custom_call_target="tpu_custom_call" | custom-call | tf_op jit(solution)/shard_map/forward/pallas_call | solution.py:484
  38.7 15.2 %all_to_all.31 = f32[32,2,128]{2,1,0:T(2,128)S(1)} all-to-all(f32[32,2,128]{2,1,0:T(2,128)S(1)} %bitcast.17), channel_id=1, replica_groups=mesh['sens'=8,'pts'=32] {'pts'}, dimensions={0} | all-to-all | bytes 65536 | tf_op jit(solution)/shard_map/all_to_all | solution.py:433
  54.0 0.0 copy-done.1
  54.0 0.0 copy-done.2
  54.0 0.0 copy-done.3
  54.0 0.0 copy-done.4
  54.0 1.4 %sensor.1 = f32[64,128]{1,0:T(8,128)S(1)} custom-call(f32[64,128]{1,0:T(8,128)S(1)} %bitcast.15, f32[2]{0:T(128)S(1)} %copy-done.4, bf16[128,1024]{1,0:T(8,128)(2,1)S(1)} %copy-done.1, bf16[1024,64]{1,0:T(8,128)(2,1)S(1)} %copy-done.3, f32[2,32,512]{2,1,0:T(8,128)S(1)} %copy-done.2), custom_call_target="tpu_custom_call" | custom-call | tf_op jit(solution)/shard_map/sensor/pallas_call | solution.py:499
  55.4 12.8 %all_to_all.32 = f32[32,2,128]{2,1,0:T(2,128)S(1)} all-to-all(f32[32,2,128]{2,1,0:T(2,128)S(1)} %bitcast.16), channel_id=1, replica_groups=mesh['sens'=8,'pts'=32] {'pts'}, dimensions={0} | all-to-all | bytes 65536 | tf_op jit(solution)/shard_map/all_to_all | solution.py:433
  68.1 0.0 copy-start
  68.1 2.7 %adjoint.1 = f32[8,128,128]{2,1,0:T(8,128)S(1)} custom-call(f32[64,128]{1,0:T(8,128)S(1)} %bitcast.14, f32[1024,128]{1,0:T(8,128)S(1)} %bitcast.12, bf16[2,14,64,1024]{3,2,1,0:T(8,128)(2,1)S(1)} %get-tuple-element.10.highs, bf16[2,14,64,1024]{3,2,1,0:T(8,128)(2,1)S(1)} %get-tuple-element.11.lows, bf16[8,256,256]{2,1,0:T(8,128)(2,1)S(1)} %get-tuple-element.12.scatter), custom_call_target="tpu_custom_call" | custom-call | tf_op jit(solution)/shard_map/adjoint/pallas_call | solution.py:507
  70.9 12.8 %all_to_all.33 = f32[8,128,128]{2,1,0:T(8,128)S(1)} all-to-all(f32[8,128,128]{2,1,0:T(8,128)S(1)} %adjoint.1), channel_id=1, replica_groups=mesh['sens'=8,'pts'=32] {'sens'}, dimensions={0} | all-to-all | bytes 1048576 | tf_op jit(solution)/shard_map/all_to_all | solution.py:433
  83.7 14.7 %all_to_all.34 = f32[32,4,128]{2,1,0:T(4,128)S(1)} all-to-all(f32[32,4,128]{2,1,0:T(4,128)S(1)} %bitcast.18), channel_id=1, replica_groups=mesh['sens'=8,'pts'=32] {'pts'}, dimensions={0} | all-to-all | bytes 131072 | tf_op jit(solution)/shard_map/all_to_all | solution.py:433
  98.4 0.6 gradient.1
  99.0 8.4 %all_to_all.35.received = f32[8,56,128]{2,1,0:T(8,128)S(1)} all-to-all(f32[8,56,128]{2,1,0:T(8,128)S(1)} %gradient.1), channel_id=1, replica_groups=mesh['sens'=8,'pts'=32] {'sens'}, dimensions={0} | all-to-all | bytes 458752 | tf_op jit(solution)/shard_map/all_to_all | solution.py:433
  107.5 0.0 copy-done
  107.5 0.8 final.1
  (1 shorter events, 0.0 us)
Async XLA Ops:
  31.6 22.3 %copy-start.1 = (bf16[128,1024]{1,0:T(8,128)(2,1)S(1)}, bf16[128,1024]{1,0:T(8,128)(2,1)}, u32[]{:S(2)}) copy-start(bf16[128,1024]{1,0:T(8,128)(2,1)} %constant.12.clone.to_time) | copy-start | bytes 786436
  31.6 22.3 %copy-start.2 = (f32[2,32,512]{2,1,0:T(8,128)S(1)}, f32[2,32,512]{2,1,0:T(8,128)}, u32[]{:S(2)}) copy-start(f32[2,32,512]{2,1,0:T(8,128)} %constant.14.clone.fine) | copy-start | bytes 393220
  31.7 22.3 %copy-start.3 = (bf16[1024,64]{1,0:T(8,128)(2,1)S(1)}, bf16[1024,64]{1,0:T(8,128)(2,1)}, u32[]{:S(2)}) copy-start(bf16[1024,64]{1,0:T(8,128)(2,1)} %constant.13.clone.to_frequency) | copy-start | bytes 393220
  31.7 22.3 %copy-start.4 = (f32[2]{0:T(128)S(1)}, f32[2]{0:T(128)}, u32[]{:S(2)}) copy-start(f32[2]{0:T(128)} %noise.1) | copy-start | bytes 28
  68.1 39.4 %copy-start = (f32[4,32,420]{2,1,0:T(8,128)S(1)}, f32[4,32,420]{2,1,0:T(8,128)}, u32[]{:S(2)}) copy-start(f32[4,32,420]{2,1,0:T(8,128)} %vectors.3) | copy-start | bytes 645124

commit v5 on v4

--- a/solution.py
+++ b/solution.py
@@ -280,7 +280,7 @@
     weight = frequency_weight(block, blocks, length)
 
     def each(n, v, values):
-        weighted = values * noise[n]
+        weighted = values * noise[:, n : n + 1]
         for half in range(2):
             high, low = halves(weighted * fine[half])
             at = slice(half * padded_time, (half + 1) * padded_time)
@@ -409,7 +409,6 @@
 
 
 VMEM = pl.BlockSpec(memory_space=pltpu.VMEM)
-SMEM = pl.BlockSpec(memory_space=pltpu.SMEM)
 HBM = pl.BlockSpec(memory_space=pltpu.HBM)
 
 
@@ -500,9 +499,9 @@
         partial(sensor_kernel, block, length),
         "sensor",
         [((sensors, LANES), f32)],
-        [VMEM, SMEM, VMEM, VMEM, VMEM],
+        [VMEM, VMEM, VMEM, VMEM, VMEM],
         [pltpu.VMEM((2 * SPAN, 2 * padded_time), bf16)],
-    )(data, noise_prec, to_time, to_frequency, fine)
+    )(data, near_core(noise_prec.reshape(1, -1)), to_time, to_frequency, fine)
     back = near_core(exchange(back.reshape(blocks, sensors // blocks, LANES), "pts").reshape(sensors, LANES))
     partial_sums = call(
         partial(adjoint_kernel, near, degree),

time: 109 us -> 108 us (level)
  no operation moved by 1% of the time
where the time goes in v5:
time: 108 us
  blocking collectives  93.2 us (86%)
  Pallas kernels  14.5 us (13%)
    all_to_all x6, blocking collectives, exchange(): return lax.all_to_all(values, axis, 0, 0, tiled=True)  93.2 us
    pallas_call x1, Pallas kernels, body(): call(partial(forward_kernel, near, degree), 'forward', [((sensors, LANES)...  7.06 us
    pallas_call x1, Pallas kernels, body(): call(partial(adjoint_kernel, near, degree), 'adjoint', [((groups, all_poi...  2.73 us
    pallas_call x1, Pallas kernels, body(): call(source_kernel, 'source', [((blocks, points, LANES), f32)], [VMEM] *...  2.42 us

profile of v5, /device:TPU:1, one launch (start us, length us, event | category | flops | bytes accessed | tf_op | source)
XLA Modules:
  0.0 107.7 jit_solution(4008426501880691304)
XLA Ops:
  0.0 2.4 %source.1 = f32[32,32,128]{2,1,0:T(8,128)S(1)} custom-call(f32[4,32,420]{2,1,0:T(8,128)} %vectors.3, f32[6,32]{1,0:T(8,128)} %bitcast.21, s32[6,32]{1,0:T(8,128)} %bitcast.22, f32[1,32]{1,0:T(1,128)} %bitcast.23, f32[1,5]{1,0:T(1,128)} %bitcast.24, bf16[432,1024]{1,0:T(8,128)(2,1)} %constant.15.clone.full_high, bf16[432,1024]{1,0:T(8,128)(2,1)} %constant.16.clone.full_low), custom_call_target="tpu_custom_call" | custom-call | tf_op jit(solution)/shard_map/source/pallas_call | solution.py:462
  2.4 29.2 %all_to_all.30 = f32[32,32,128]{2,1,0:T(8,128)S(1)} all-to-all(f32[32,32,128]{2,1,0:T(8,128)S(1)} %source.1), channel_id=1, replica_groups=mesh['sens'=8,'pts'=32] {'pts'}, dimensions={0} | all-to-all | bytes 1048576 | tf_op jit(solution)/shard_map/all_to_all | solution.py:432
  31.6 0.0 copy-start.1
  31.6 0.0 copy-start.2
  31.7 0.0 copy-start.3
  31.7 0.0 copy-start.4
  31.7 7.1 %forward.1 = (f32[64,128]{1,0:T(8,128)S(1)}, bf16[2,14,64,1024]{3,2,1,0:T(8,128)(2,1)S(1)}, bf16[2,14,64,1024]{3,2,1,0:T(8,128)(2,1)S(1)}, bf16[8,256,256]{2,1,0:T(8,128)(2,1)S(1)}) custom-call(f32[1024,128]{1,0:T(8,128)S(1)} %bitcast.12, f32[2,14,64,1024]{3,2,1,0:T(8,128)} %kernel.1), custom_call_target="tpu_custom_call" | custom-call | tf_op jit(solution)/shard_map/forward/pallas_call | solution.py:483
  38.7 15.2 %all_to_all.31 = f32[32,2,128]{2,1,0:T(2,128)S(1)} all-to-all(f32[32,2,128]{2,1,0:T(2,128)S(1)} %bitcast.18), channel_id=1, replica_groups=mesh['sens'=8,'pts'=32] {'pts'}, dimensions={0} | all-to-all | bytes 65536 | tf_op jit(solution)/shard_map/all_to_all | solution.py:432
  54.0 0.0 copy-done.1
  54.0 0.0 copy-done.2
  54.0 0.0 copy-done.3
  54.0 0.0 copy-done.4
  54.0 0.8 sensor.1
  54.8 12.8 %all_to_all.32 = f32[32,2,128]{2,1,0:T(2,128)S(1)} all-to-all(f32[32,2,128]{2,1,0:T(2,128)S(1)} %bitcast.17), channel_id=1, replica_groups=mesh['sens'=8,'pts'=32] {'pts'}, dimensions={0} | all-to-all | bytes 65536 | tf_op jit(solution)/shard_map/all_to_all | solution.py:432
  67.6 0.0 copy-start
  67.6 2.7 %adjoint.1 = f32[8,128,128]{2,1,0:T(8,128)S(1)} custom-call(f32[64,128]{1,0:T(8,128)S(1)} %bitcast.15, f32[1024,128]{1,0:T(8,128)S(1)} %bitcast.13, bf16[2,14,64,1024]{3,2,1,0:T(8,128)(2,1)S(1)} %get-tuple-element.10.highs, bf16[2,14,64,1024]{3,2,1,0:T(8,128)(2,1)S(1)} %get-tuple-element.11.lows, bf16[8,256,256]{2,1,0:T(8,128)(2,1)S(1)} %get-tuple-element.12.scatter), custom_call_target="tpu_custom_call" | custom-call | tf_op jit(solution)/shard_map/adjoint/pallas_call | solution.py:506
  70.3 12.8 %all_to_all.33 = f32[8,128,128]{2,1,0:T(8,128)S(1)} all-to-all(f32[8,128,128]{2,1,0:T(8,128)S(1)} %adjoint.1), channel_id=1, replica_groups=mesh['sens'=8,'pts'=32] {'sens'}, dimensions={0} | all-to-all | bytes 1048576 | tf_op jit(solution)/shard_map/all_to_all | solution.py:432
  83.2 14.7 %all_to_all.34 = f32[32,4,128]{2,1,0:T(4,128)S(1)} all-to-all(f32[32,4,128]{2,1,0:T(4,128)S(1)} %bitcast.20), channel_id=1, replica_groups=mesh['sens'=8,'pts'=32] {'pts'}, dimensions={0} | all-to-all | bytes 131072 | tf_op jit(solution)/shard_map/all_to_all | solution.py:432
  97.9 0.6 gradient.1
  98.5 8.4 %all_to_all.35.received = f32[8,56,128]{2,1,0:T(8,128)S(1)} all-to-all(f32[8,56,128]{2,1,0:T(8,128)S(1)} %gradient.1), channel_id=1, replica_groups=mesh['sens'=8,'pts'=32] {'sens'}, dimensions={0} | all-to-all | bytes 458752 | tf_op jit(solution)/shard_map/all_to_all | solution.py:432
  107.0 0.0 copy-done
  107.0 0.8 final.1
  (1 shorter events, 0.0 us)
Async XLA Ops:
  31.6 22.3 %copy-start.1 = (bf16[128,1024]{1,0:T(8,128)(2,1)S(1)}, bf16[128,1024]{1,0:T(8,128)(2,1)}, u32[]{:S(2)}) copy-start(bf16[128,1024]{1,0:T(8,128)(2,1)} %constant.12.clone.to_time) | copy-start | bytes 786436
  31.6 22.3 %copy-start.2 = (f32[2,32,512]{2,1,0:T(8,128)S(1)}, f32[2,32,512]{2,1,0:T(8,128)}, u32[]{:S(2)}) copy-start(f32[2,32,512]{2,1,0:T(8,128)} %constant.14.clone.fine) | copy-start | bytes 393220
  31.7 22.3 %copy-start.3 = (bf16[1024,64]{1,0:T(8,128)(2,1)S(1)}, bf16[1024,64]{1,0:T(8,128)(2,1)}, u32[]{:S(2)}) copy-start(bf16[1024,64]{1,0:T(8,128)(2,1)} %constant.13.clone.to_frequency) | copy-start | bytes 393220
  31.7 22.3 %copy-start.4 = (f32[2]{0:T(128)S(1)}, f32[2]{0:T(128)}, u32[]{:S(2)}) copy-start(f32[2]{0:T(128)} %param.14) | copy-start | bytes 28
  67.6 39.4 %copy-start = (f32[4,32,420]{2,1,0:T(8,128)S(1)}, f32[4,32,420]{2,1,0:T(8,128)}, u32[]{:S(2)}) copy-start(f32[4,32,420]{2,1,0:T(8,128)} %vectors.3) | copy-start | bytes 645124
